TPU v7x, 512 devices: a whole 4x4x16 slice. The times are simulated.
512 devices in a mesh: tm: 32 (over x, z_lo), height: 8 (over z_hi, y), dp: 2 (over core).
Axes of the slice: x: 4, y: 4, z: 16 (z_hi: 2, z_lo: 8; z = z_hi * 8 + z_lo), core: 2. Of those that a mesh axis runs over, the one named last changes fastest.
Arguments:
- frames_in: bfloat16 [2, 128, 32, 48, 256], P('dp', 'tm', 'height'), may hold values from -6 to 6
- cotangent: bfloat16 [2, 128, 32, 48, 256], P('dp', 'tm', 'height'), may hold values from -6 to 6
- w_spatial: bfloat16 [3, 3, 256, 256], replicated, may hold values from -0.125 to 0.125
- w_temporal: bfloat16 [3, 256, 256], replicated, may hold values from -0.21875 to 0.21875
Outputs:
- decoded: bfloat16 [2, 128, 32, 48, 256], P('dp', 'tm', 'height')
- input_grad: bfloat16 [2, 128, 32, 48, 256], P('dp', 'tm', 'height')
- spatial_grad: bfloat16 [3, 3, 256, 256], replicated
- temporal_grad: bfloat16 [3, 256, 256], replicated
All inputs are finite; a program needn't handle non-finite values.
Results may differ from a plain program's by a relative error of at most 0.0061.
Values may be sent and summed in bfloat16 or wider, within the bound.
No kernel may reach another device: no remote copies, remote signals or barrier semaphores. Data moves between devices by JAX's collectives and lax.ppermute only.
A program may use at most 64 MiB of HBM per device.

v0:
```python
import math

import jax
import jax.numpy as jnp
from jax import lax
from jax.sharding import PartitionSpec as P


def extended(x, sides, width):
    for axis, dim in sides:
        count, length = (lax.axis_size(axis), x.shape[dim])
        up = [(i, (i + 1) % count) for i in range(count - 1)]
        down = [(j, i) for i, j in up]
        last = lax.slice_in_dim(x, length - width, length, axis=dim)
        initial = lax.slice_in_dim(x, 0, width, axis=dim)
        before = lax.ppermute(last, axis, up)
        after = lax.ppermute(initial, axis, down)
        x = jnp.concatenate([before, x, after], axis=dim)
    return x


def from_behind(block, axis, distance):
    devices = range(lax.axis_size(axis))
    route = [(i - distance, i) for i in devices if i - distance in devices]
    return lax.ppermute(block, axis, route)


def silu_slope(values):
    sigmoid_value = jax.nn.sigmoid(values)
    return sigmoid_value * (1.0 + values * (1.0 - sigmoid_value))


def forward_taps(padded, row_count, col_count):
    pieces = [
        padded[:, row_tap : row_tap + row_count, col_tap : col_tap + col_count]
        for row_tap in range(3)
        for col_tap in range(3)
    ]
    return jnp.concatenate(pieces, axis=-1)


def backward_taps(padded, row_count, col_count):
    pieces = [
        padded[:, 2 - row_tap : 2 - row_tap + row_count, 2 - col_tap : 2 - col_tap + col_count]
        for row_tap in range(3)
        for col_tap in range(3)
    ]
    return jnp.concatenate(pieces, axis=-1)


def frame_taps(source, frame_count):
    return jnp.concatenate(
        [source[shift_tap : shift_tap + frame_count] for shift_tap in range(3)], axis=-1
    )


def flat_dot(left_side, right_side):
    return jnp.dot(
        left_side.reshape(-1, left_side.shape[-1]), right_side, preferred_element_type=jnp.float32
    )


def local(frames_in, cotangent, w_spatial, w_temporal):
    inputs = frames_in[0]
    upstream = cotangent[0]
    frame_count, row_count, col_count, channels = inputs.shape
    spatial_flat = w_spatial.reshape(9 * channels, channels)
    temporal_flat = w_temporal.reshape(3 * channels, channels)
    spatial_back = jnp.concatenate(
        [w_spatial[row_tap, col_tap].T for row_tap in range(3) for col_tap in range(3)], axis=0
    )
    temporal_back = jnp.concatenate([w_temporal[2].T, w_temporal[1].T, w_temporal[0].T], axis=0)
    first_shard = lax.axis_index("tm") == 0
    activated = jax.nn.silu(inputs.astype(jnp.float32)).astype(jnp.bfloat16)
    activ_rows = extended(activated, (("height", 1),), 1)
    activ_pad = jnp.pad(activ_rows, ((0, 0), (0, 0), (1, 1), (0, 0)))
    activ_taps = forward_taps(activ_pad, row_count, col_count).reshape(-1, 9 * channels)
    spatial_out = jnp.dot(activ_taps, spatial_flat, preferred_element_type=jnp.float32)
    spatial_out = spatial_out.astype(jnp.bfloat16).reshape(inputs.shape)
    earlier = from_behind(spatial_out[frame_count - 2 :], "tm", 1)
    repeated = jnp.broadcast_to(spatial_out[:1], earlier.shape)
    earlier = jnp.where(first_shard, repeated, earlier)
    padded_frames = jnp.concatenate([earlier, spatial_out], axis=0)
    frame_stack = frame_taps(padded_frames, frame_count).reshape(-1, 3 * channels)
    temporal_out = jnp.dot(frame_stack, temporal_flat, preferred_element_type=jnp.float32).reshape(
        inputs.shape
    )
    decoded = (inputs.astype(jnp.float32) + temporal_out).astype(jnp.bfloat16)
    upstream_ext = jnp.pad(upstream, ((2, 2), (0, 0), (0, 0), (0, 0)))
    frame_part = flat_dot(frame_taps(upstream_ext, frame_count + 2), temporal_back)
    frame_part = frame_part.reshape(frame_count + 2, row_count, col_count, channels)
    rim_part = frame_part[:2]
    returned = from_behind(rim_part, "tm", -1)
    frame_sum = frame_part[2:]
    frame_sum = frame_sum.at[frame_count - 2 :].add(returned)
    frame_sum = frame_sum.at[0].add(jnp.where(first_shard, rim_part[0] + rim_part[1], 0.0))
    frame_grad = frame_sum.astype(jnp.bfloat16)
    grad_pad = jnp.pad(frame_grad, ((0, 0), (2, 2), (1, 1), (0, 0)))
    grad_ext = flat_dot(backward_taps(grad_pad, row_count + 2, col_count), spatial_back)
    grad_ext = grad_ext.reshape(frame_count, row_count + 2, col_count, channels)
    edge_rows = jnp.stack([grad_ext[:, 0], grad_ext[:, row_count + 1]], axis=1)
    arrived = extended(edge_rows.astype(jnp.bfloat16), (("height", 1),), 1).astype(edge_rows.dtype)
    act_grad = grad_ext[:, 1 : row_count + 1]
    act_grad = act_grad.at[:, 0].add(arrived[:, 0])
    act_grad = act_grad.at[:, row_count - 1].add(arrived[:, 3])
    input_grad = (
        upstream.astype(jnp.float32) + silu_slope(inputs.astype(jnp.float32)) * act_grad
    ).astype(jnp.bfloat16)
    cell_count = (
        frame_count
        * lax.axis_size("tm")
        * row_count
        * lax.axis_size("height")
        * col_count
        * lax.axis_size("dp")
    )
    grad_scale = 1.0 / math.sqrt(cell_count)
    contract = (((0,), (0,)), ((), ()))
    spatial_term = lax.dot_general(
        activ_taps, frame_grad.reshape(-1, channels), contract, preferred_element_type=jnp.float32
    )
    temporal_term = lax.dot_general(
        frame_stack, upstream.reshape(-1, channels), contract, preferred_element_type=jnp.float32
    )
    weight_terms = jnp.concatenate([spatial_term, temporal_term], axis=0) * grad_scale
    summed = lax.psum(weight_terms, ("tm", "height", "dp")).astype(jnp.bfloat16)
    spatial_grad = summed[: 9 * channels].reshape(3, 3, channels, channels)
    temporal_grad = summed[9 * channels :].reshape(3, channels, channels)
    return (decoded[None], input_grad[None], spatial_grad, temporal_grad)


def solution(mesh):
    return jax.shard_map(
        local,
        mesh=mesh,
        in_specs=(
            P("dp", "tm", "height", None, None),
            P("dp", "tm", "height", None, None),
            P(),
            P(),
        ),
        out_specs=(
            P("dp", "tm", "height", None, None),
            P("dp", "tm", "height", None, None),
            P(),
            P(),
        ),
        check_vma=False,
    )
```

profile of v0, /device:TPU:7, one launch (start us, length us, event | category | flops | bytes accessed | tf_op | source)
XLA Modules:
  0.0 287.3 jit_solution(785562103229142495)
XLA Ops:
  0.6 0.0 copy-start.7
  0.6 1.5 pad_slice_fusion.11
  2.2 0.1 pad_maximum_fusion
  2.4 0.7 fusion.42
  3.0 0.8 fusion.57
  3.8 13.1 %collective-permute-start.3 = (f32[2,4,48,256]{3,2,1,0:T(8,128)}, f32[2,4,48,256]{3,2,1,0:T(8,128)}, u32[]{:S(2)}, u32[]{:S(2)}) collective-permute-start(f32[2,4,48,256]{3,2,1,0:T(8,128)} %bitcast.21), channel_id=1, source_target_pairs={{16,0},{32,16},{48,32},{64,48},{80,64},{96,80},{112,96},{128,112},... | collective-permute-start | bytes 1179656 | tf_op jit(solution)/shard_map/ppermute | solution.py:25
  17.0 0.1 slice.352
  17.1 1.0 fusion.56
  18.1 1.0 copy.20
  19.1 0.7 bitcast_dynamic-update-slice_fusion.8
  19.8 1.0 copy.21
  20.8 1.0 copy.22
  21.8 1.0 copy.23
  22.8 1.0 copy.24
  23.8 1.0 copy.25
  24.8 1.0 copy.26
  25.8 1.0 copy.27
  26.9 0.1 copy.28
  27.0 0.7 bitcast_dynamic-update-slice_fusion.7
  27.6 0.7 bitcast_dynamic-update-slice_fusion.6
  28.3 0.7 bitcast_dynamic-update-slice_fusion.5
  29.0 0.7 bitcast_dynamic-update-slice_fusion.4
  29.6 0.7 bitcast_dynamic-update-slice_fusion.3
  30.3 0.7 bitcast_dynamic-update-slice_fusion.2
  31.0 0.7 bitcast_dynamic-update-slice_fusion.1
  31.6 0.7 bitcast_dynamic-update-slice_fusion
  32.3 1.0 add_dynamic-update-slice_fusion
  33.5 0.1 fusion.30
  33.6 0.1 fusion.32
  33.8 0.1 fusion.33
  34.0 0.1 fusion.35
  34.1 0.1 fusion.36
  34.3 0.1 fusion.38
  34.4 0.8 copy-done.13
  35.2 1.6 fusion.60
  36.8 3.3 %collective-permute-start.4 = (bf16[4,1,48,256]{3,2,1,0:T(8,128)(2,1)S(1)}, bf16[4,1,48,256]{3,2,1,0:T(8,128)(2,1)S(1)}, u32[]{:S(2)}, u32[]{:S(2)}) collective-permute-start(bf16[4,1,48,256]{3,2,1,0:T(8,128)(2,1)S(1)} %get-tuple-element.63), channel_id=1, source_target_pairs={{0,2},{2,4},{4,6},{6,8},{8,10},{10,12},{12,14},{1,3},{3,5},{5,7},{... | collective-permute-start | bytes 294920 | tf_op jit(solution)/shard_map/ppermute | solution.py:16
  40.1 1.3 collective-permute-start.5
  41.4 0.1 slice.358
  41.5 0.2 collective-permute-done.4
  41.8 3.7 %collective-permute-done.5 = bf16[4,1,48,256]{3,2,1,0:T(8,128)(2,1)S(1)} collective-permute-done((bf16[4,1,48,256]{3,2,1,0:T(8,128)(2,1)S(1)}, bf16[4,1,48,256]{3,2,1,0:T(8,128)(2,1)S(1)}, u32[]{:S(2)}, u32[]{:S(2)}) %collective-permute-start.5) | collective-permute-done | bytes 98336 | tf_op jit(solution)/shard_map/ppermute | solution.py:17
  45.6 1.1 fusion.48
  46.7 3.2 %collective-permute-start = (bf16[4,1,48,256]{3,2,1,0:T(8,128)(2,1)S(1)}, bf16[4,1,48,256]{3,2,1,0:T(8,128)(2,1)S(1)}, u32[]{:S(2)}, u32[]{:S(2)}) collective-permute-start(bf16[4,1,48,256]{3,2,1,0:T(8,128)(2,1)S(1)} %get-tuple-element.75), channel_id=1, source_target_pairs={{0,2},{2,4},{4,6},{6,8},{8,10},{10,12},{12,14},{1,3},{3,5},{5,7},{... | collective-permute-start | bytes 294920 | tf_op jit(solution)/shard_map/ppermute | solution.py:16
  50.0 1.3 collective-permute-start.1
  51.3 0.3 collective-permute-done
  51.6 7.5 %collective-permute-done.1 = bf16[4,1,48,256]{3,2,1,0:T(8,128)(2,1)S(1)} collective-permute-done((bf16[4,1,48,256]{3,2,1,0:T(8,128)(2,1)S(1)}, bf16[4,1,48,256]{3,2,1,0:T(8,128)(2,1)S(1)}, u32[]{:S(2)}, u32[]{:S(2)}) %collective-permute-start.1) | collective-permute-done | bytes 98336 | tf_op jit(solution)/shard_map/ppermute | solution.py:17
  59.1 0.3 fusion.29
  59.5 0.1 slice_dynamic-update-slice_fusion.4
  59.7 0.2 constant_dynamic-update-slice_fusion
  59.9 0.1 slice_dynamic-update-slice_fusion.2
  60.1 0.1 slice_dynamic-update-slice_fusion
  60.2 0.7 copy-done.5
  60.9 1.1 convolution_convert_fusion
  62.0 1.9 collective-permute-start.2
  63.9 1.2 convolution_bitcast_fusion
  65.1 10.8 %collective-permute-done.2 = bf16[2,4,48,256]{3,2,1,0:T(8,128)(2,1)S(1)} collective-permute-done((bf16[2,4,48,256]{3,2,1,0:T(8,128)(2,1)S(1)}, bf16[2,4,48,256]{3,2,1,0:T(8,128)(2,1)S(1)}, u32[]{:S(2)}, u32[]{:S(2)}) %collective-permute-start.2) | collective-permute-done | bytes 196640 | tf_op jit(solution)/shard_map/ppermute | solution.py:25
  76.0 0.1 fusion.39
  76.0 0.7 copy-done.9
  76.8 0.1 copy-done.11
  76.9 0.5 fusion.8
  77.4 0.3 maximum_multiply_fusion
  77.7 204.1 %all-reduce.4 = bf16[3072,256]{1,0:T(8,128)(2,1)} all-reduce(f32[3072,256]{1,0:T(8,128)S(1)} %maximum_multiply_fusion), channel_id=1, replica_groups=mesh['tm'=32,'height'=8,'dp'=2] {'tm','height','dp'}, use_global_device_ids=true, to_apply=%region_0.1 | all-reduce | flops 786432 | bytes 4718592 | tf_op jit(solution)/shard_map/psum | solution.py:126
  281.8 2.5 slice.363
  284.3 1.8 slice.364
  286.1 1.2 fusion.2
  (43 shorter events, 0.6 us)
Async XLA Ops:
  0.6 1.6 copy-start.7
  3.0 14.0 %copy-start.4 = (bf16[3,3,256,256]{3,2,1,0:T(8,128)(2,1)S(1)}, bf16[3,3,256,256]{3,2,1,0:T(8,128)(2,1)}, u32[]{:S(2)}) copy-start(bf16[3,3,256,256]{3,2,1,0:T(8,128)(2,1)} %param.14) | copy-start | bytes 3538948
  3.8 28.5 %collective-permute-start.3 = (f32[2,4,48,256]{3,2,1,0:T(8,128)}, f32[2,4,48,256]{3,2,1,0:T(8,128)}, u32[]{:S(2)}, u32[]{:S(2)}) collective-permute-start(f32[2,4,48,256]{3,2,1,0:T(8,128)} %bitcast.21), channel_id=1, source_target_pairs={{16,0},{32,16},{48,32},{64,48},{80,64},{96,80},{112,96},{128,112},... | collective-permute-start | bytes 1179656 | tf_op jit(solution)/shard_map/ppermute | solution.py:25
  18.1 8.8 %copy-start.6 = (bf16[1,1,256,256]{3,2,1,0:T(8,128)(2,1)S(1)}, bf16[1,1,256,256]{3,2,1,0:T(8,128)(2,1)}, u32[]{:S(2)}) copy-start(bf16[1,1,256,256]{3,2,1,0:T(8,128)(2,1)} %get-tuple-element.52) | copy-start | bytes 393220
  33.9 1.3 copy-start.13
  36.8 8.8 %copy-start = (bf16[1,4,4,48,256]{4,3,2,1,0:T(8,128)(2,1)S(1)}, bf16[1,4,4,48,256]{4,3,2,1,0:T(8,128)(2,1)}, u32[]{:S(2)}) copy-start(bf16[1,4,4,48,256]{4,3,2,1,0:T(8,128)(2,1)} %param.12) | copy-start | bytes 1179652
  36.8 8.8 %copy-start.1 = (bf16[1,4,4,48,256]{4,3,2,1,0:T(8,128)(2,1)S(1)}, bf16[1,4,4,48,256]{4,3,2,1,0:T(8,128)(2,1)}, u32[]{:S(2)}) copy-start(bf16[1,4,4,48,256]{4,3,2,1,0:T(8,128)(2,1)} %param.13) | copy-start | bytes 1179652
  36.8 5.0 %collective-permute-start.4 = (bf16[4,1,48,256]{3,2,1,0:T(8,128)(2,1)S(1)}, bf16[4,1,48,256]{3,2,1,0:T(8,128)(2,1)S(1)}, u32[]{:S(2)}, u32[]{:S(2)}) collective-permute-start(bf16[4,1,48,256]{3,2,1,0:T(8,128)(2,1)S(1)} %get-tuple-element.63), channel_id=1, source_target_pairs={{0,2},{2,4},{4,6},{6,8},{8,10},{10,12},{12,14},{1,3},{3,5},{5,7},{... | collective-permute-start | bytes 294920 | tf_op jit(solution)/shard_map/ppermute | solution.py:16
  40.1 5.4 %collective-permute-start.5 = (bf16[4,1,48,256]{3,2,1,0:T(8,128)(2,1)S(1)}, bf16[4,1,48,256]{3,2,1,0:T(8,128)(2,1)S(1)}, u32[]{:S(2)}, u32[]{:S(2)}) collective-permute-start(bf16[4,1,48,256]{3,2,1,0:T(8,128)(2,1)S(1)} %get-tuple-element.64), channel_id=1, source_target_pairs={{2,0},{4,2},{6,4},{8,6},{10,8},{12,10},{14,12},{3,1},{5,3},{7,5},{... | collective-permute-start | bytes 294920 | tf_op jit(solution)/shard_map/ppermute | solution.py:17
  46.7 4.8 %collective-permute-start = (bf16[4,1,48,256]{3,2,1,0:T(8,128)(2,1)S(1)}, bf16[4,1,48,256]{3,2,1,0:T(8,128)(2,1)S(1)}, u32[]{:S(2)}, u32[]{:S(2)}) collective-permute-start(bf16[4,1,48,256]{3,2,1,0:T(8,128)(2,1)S(1)} %get-tuple-element.75), channel_id=1, source_target_pairs={{0,2},{2,4},{4,6},{6,8},{8,10},{10,12},{12,14},{1,3},{3,5},{5,7},{... | collective-permute-start | bytes 294920 | tf_op jit(solution)/shard_map/ppermute | solution.py:16
  50.0 9.1 %collective-permute-start.1 = (bf16[4,1,48,256]{3,2,1,0:T(8,128)(2,1)S(1)}, bf16[4,1,48,256]{3,2,1,0:T(8,128)(2,1)S(1)}, u32[]{:S(2)}, u32[]{:S(2)}) collective-permute-start(bf16[4,1,48,256]{3,2,1,0:T(8,128)(2,1)S(1)} %get-tuple-element.76), channel_id=1, source_target_pairs={{2,0},{4,2},{6,4},{8,6},{10,8},{12,10},{14,12},{3,1},{5,3},{7,5},{... | collective-permute-start | bytes 294920 | tf_op jit(solution)/shard_map/ppermute | solution.py:17
  59.6 1.3 copy-start.5
  62.0 14.1 %copy-start.2 = (bf16[768,256]{1,0:T(8,128)(2,1)}, bf16[768,256]{1,0:T(8,128)(2,1)S(1)}, u32[]{:S(2)}) copy-start(bf16[768,256]{1,0:T(8,128)(2,1)S(1)} %convolution_convert_fusion) | copy-start | bytes 1179652
  62.0 13.9 %collective-permute-start.2 = (bf16[2,4,48,256]{3,2,1,0:T(8,128)(2,1)S(1)}, bf16[2,4,48,256]{3,2,1,0:T(8,128)(2,1)S(1)}, u32[]{:S(2)}, u32[]{:S(2)}) collective-permute-start(bf16[2,4,48,256]{3,2,1,0:T(8,128)(2,1)S(1)} %bitcast.117), channel_id=1, source_target_pairs={{0,16},{16,32},{32,48},{48,64},{64,80},{80,96},{96,112},{112,128},... | collective-permute-start | bytes 589832 | tf_op jit(solution)/shard_map/ppermute | solution.py:25
  76.0 0.7 copy-start.9
  76.0 0.9 copy-start.11
  281.8 4.3 %copy-start.3 = (bf16[768,256]{1,0:T(8,128)(2,1)S(1)}, bf16[768,256]{1,0:T(8,128)(2,1)}, u32[]{:S(2)}) copy-start(bf16[768,256]{1,0:T(8,128)(2,1)} %copy-done.2) | copy-start | bytes 1179652
  281.8 4.3 %copy-start.8 = (bf16[3,256,256]{2,1,0:T(8,128)(2,1)S(1)}, bf16[3,256,256]{2,1,0:T(8,128)(2,1)}, u32[]{:S(2)}) copy-start(bf16[3,256,256]{2,1,0:T(8,128)(2,1)} %param.15) | copy-start | bytes 1179652
  281.8 4.3 %copy-start.10 = (bf16[4,4,48,256]{3,2,1,0:T(8,128)(2,1)S(1)}, bf16[4,4,48,256]{3,2,1,0:T(8,128)(2,1)}, u32[]{:S(2)}) copy-start(bf16[4,4,48,256]{3,2,1,0:T(8,128)(2,1)} %copy-done.9) | copy-start | bytes 1179652
  281.8 4.3 %copy-start.12 = (bf16[4,4,48,256]{3,2,1,0:T(8,128)(2,1)S(1)}, bf16[4,4,48,256]{3,2,1,0:T(8,128)(2,1)}, u32[]{:S(2)}) copy-start(bf16[4,4,48,256]{3,2,1,0:T(8,128)(2,1)} %copy-done.11) | copy-start | bytes 1179652
where the time goes:
time: 289 us; the launch traced here: 287 us
  blocking collectives  204 us (71%)
  local copies, waits for them, and re-layouts  25.6 us (9%)
  starting transfers between devices  24.2 us (8%)
  waiting for transfers between devices  22.6 us (8%)
  matrix products  6.2 us (2%)
  other arithmetic  3.42 us (1%)
    psum x1, blocking collectives, local(): summed = lax.psum(weight_terms, ('tm', 'height', 'dp')).astype(jnp.bfloat16)  204 us
    unnamed x58, local copies, waits for them, and re-layouts  16.9 us
    ppermute x2, starting transfers between devices, from_behind(): return lax.ppermute(block, axis, route)  15.1 us
    ppermute x2, waiting for transfers between devices, extended(): after = lax.ppermute(initial, axis, down)  11.3 us
    ppermute x2, waiting for transfers between devices, from_behind(): return lax.ppermute(block, axis, route)  10.8 us
    ppermute x2, starting transfers between devices, extended(): before = lax.ppermute(last, axis, up)  6.54 us
  transfers between devices with their start and end apart: 6, of which 5 were waited for; matrix products, arithmetic and copies ran while one was open for 6% of the time, Pallas kernels for 0%

commit v1 on v0

--- a/solution.py
+++ b/solution.py
@@ -30,24 +30,6 @@
     return sigmoid_value * (1.0 + values * (1.0 - sigmoid_value))
 
 
-def forward_taps(padded, row_count, col_count):
-    pieces = [
-        padded[:, row_tap : row_tap + row_count, col_tap : col_tap + col_count]
-        for row_tap in range(3)
-        for col_tap in range(3)
-    ]
-    return jnp.concatenate(pieces, axis=-1)
-
-
-def backward_taps(padded, row_count, col_count):
-    pieces = [
-        padded[:, 2 - row_tap : 2 - row_tap + row_count, 2 - col_tap : 2 - col_tap + col_count]
-        for row_tap in range(3)
-        for col_tap in range(3)
-    ]
-    return jnp.concatenate(pieces, axis=-1)
-
-
 def frame_taps(source, frame_count):
     return jnp.concatenate(
         [source[shift_tap : shift_tap + frame_count] for shift_tap in range(3)], axis=-1
@@ -64,19 +46,16 @@
     inputs = frames_in[0]
     upstream = cotangent[0]
     frame_count, row_count, col_count, channels = inputs.shape
-    spatial_flat = w_spatial.reshape(9 * channels, channels)
     temporal_flat = w_temporal.reshape(3 * channels, channels)
-    spatial_back = jnp.concatenate(
-        [w_spatial[row_tap, col_tap].T for row_tap in range(3) for col_tap in range(3)], axis=0
-    )
     temporal_back = jnp.concatenate([w_temporal[2].T, w_temporal[1].T, w_temporal[0].T], axis=0)
     first_shard = lax.axis_index("tm") == 0
     activated = jax.nn.silu(inputs.astype(jnp.float32)).astype(jnp.bfloat16)
     activ_rows = extended(activated, (("height", 1),), 1)
     activ_pad = jnp.pad(activ_rows, ((0, 0), (0, 0), (1, 1), (0, 0)))
-    activ_taps = forward_taps(activ_pad, row_count, col_count).reshape(-1, 9 * channels)
-    spatial_out = jnp.dot(activ_taps, spatial_flat, preferred_element_type=jnp.float32)
-    spatial_out = spatial_out.astype(jnp.bfloat16).reshape(inputs.shape)
+    spatial_out = lax.conv_general_dilated(
+        activ_pad, w_spatial, (1, 1), "VALID", dimension_numbers=("NHWC", "HWIO", "NHWC"),
+        preferred_element_type=jnp.float32,
+    ).astype(jnp.bfloat16)
     earlier = from_behind(spatial_out[frame_count - 2 :], "tm", 1)
     repeated = jnp.broadcast_to(spatial_out[:1], earlier.shape)
     earlier = jnp.where(first_shard, repeated, earlier)
@@ -96,8 +75,11 @@
     frame_sum = frame_sum.at[0].add(jnp.where(first_shard, rim_part[0] + rim_part[1], 0.0))
     frame_grad = frame_sum.astype(jnp.bfloat16)
     grad_pad = jnp.pad(frame_grad, ((0, 0), (2, 2), (1, 1), (0, 0)))
-    grad_ext = flat_dot(backward_taps(grad_pad, row_count + 2, col_count), spatial_back)
-    grad_ext = grad_ext.reshape(frame_count, row_count + 2, col_count, channels)
+    spatial_flip = jnp.flip(w_spatial, (0, 1)).transpose(0, 1, 3, 2)
+    grad_ext = lax.conv_general_dilated(
+        grad_pad, spatial_flip, (1, 1), "VALID", dimension_numbers=("NHWC", "HWIO", "NHWC"),
+        preferred_element_type=jnp.float32,
+    )
     edge_rows = jnp.stack([grad_ext[:, 0], grad_ext[:, row_count + 1]], axis=1)
     arrived = extended(edge_rows.astype(jnp.bfloat16), (("height", 1),), 1).astype(edge_rows.dtype)
     act_grad = grad_ext[:, 1 : row_count + 1]
@@ -116,9 +98,10 @@
     )
     grad_scale = 1.0 / math.sqrt(cell_count)
     contract = (((0,), (0,)), ((), ()))
-    spatial_term = lax.dot_general(
-        activ_taps, frame_grad.reshape(-1, channels), contract, preferred_element_type=jnp.float32
-    )
+    spatial_term = lax.conv_general_dilated(
+        activ_pad, frame_grad, (1, 1), "VALID", dimension_numbers=("CHWN", "IHWO", "HWNC"),
+        preferred_element_type=jnp.float32,
+    ).reshape(9 * channels, channels)
     temporal_term = lax.dot_general(
         frame_stack, upstream.reshape(-1, channels), contract, preferred_element_type=jnp.float32
     )

time: 289 us -> 293 us (1.014)
  waiting for transfers between devices: 22.6 us -> 26.3 us
  other arithmetic: 3.42 us -> 6.71 us
  local copies, waits for them, and re-layouts: 25.6 us -> 22.6 us
    unnamed x58 -> x21, local copies, waits for them, and re-layouts: 16.9 us -> 0.84 us
    scatter-add x0 -> x1, local copies, waits for them, and re-layouts: none -> 6.33 us  [local(): frame_sum.at[0].add(jnp.where(first_shard, rim_part[0] + rim_part[1], 0.0))]
    conv_general_dilated x0 -> x3, matrix products: none -> 5.19 us  [the longest x1 2.13 us: local(): lax.conv_general_dilated(activ_pad, frame_grad, (1, 1), 'VALID', dimensio...]
    ppermute x2, waiting for transfers between devices: 10.8 us -> 15.9 us  [from_behind(): return lax.ppermute(block, axis, route)]
    another operation x0 -> x6, local copies, waits for them, and re-layouts: none -> 4.05 us
  transfers between devices with their start and end apart: 6 -> 6, of which waited for: 5 -> 5; matrix products, arithmetic and copies ran while one was open for 6% -> 3% of each run, Pallas kernels for 0% -> 0%
where the time goes in v1:
time: 293 us; the launch traced here: 292 us
  blocking collectives  203 us (69%)
  waiting for transfers between devices  26.3 us (9%)
  starting transfers between devices  24.2 us (8%)
  local copies, waits for them, and re-layouts  22.6 us (8%)
  matrix products  7.59 us (3%)
  other arithmetic  6.71 us (2%)
    psum x1, blocking collectives, local(): summed = lax.psum(weight_terms, ('tm', 'height', 'dp')).astype(jnp.bfloat16)  203 us
    ppermute x2, waiting for transfers between devices, from_behind(): return lax.ppermute(block, axis, route)  15.9 us
    ppermute x2, starting transfers between devices, from_behind(): return lax.ppermute(block, axis, route)  15.2 us
    ppermute x2, waiting for transfers between devices, extended(): after = lax.ppermute(initial, axis, down)  10.2 us
    ppermute x2, starting transfers between devices, extended(): before = lax.ppermute(last, axis, up)  6.42 us
    scatter-add x1, local copies, waits for them, and re-layouts, local(): frame_sum.at[0].add(jnp.where(first_shard, rim_part[0] + rim_part[1], 0.0))  6.33 us
  transfers between devices with their start and end apart: 6, of which 5 were waited for; matrix products, arithmetic and copies ran while one was open for 3% of the time, Pallas kernels for 0%

profile of v1, /device:TPU:7, one launch (start us, length us, event | category | flops | bytes accessed | tf_op | source)
XLA Modules:
  0.0 291.8 jit_solution(13264414294264656128)
XLA Ops:
  0.6 0.0 copy-start
  0.6 1.2 slice_bitcast_fusion.2
  1.8 1.5 pad_slice_fusion.2
  3.3 0.1 pad_maximum_fusion
  3.5 0.7 fusion.28
  4.1 0.1 fusion.47
  4.2 1.1 copy.24
  5.3 13.1 %collective-permute-start.3 = (f32[2,4,48,256]{3,0,2,1:T(2,128)}, f32[2,4,48,256]{3,0,2,1:T(2,128)}, u32[]{:S(2)}, u32[]{:S(2)}) collective-permute-start(f32[2,4,48,256]{3,0,2,1:T(2,128)} %copy.24), channel_id=1, source_target_pairs={{16,0},{32,16},{48,32},{64,48},{80,64},{96,80},{112,96},{128,112},... | collective-permute-start | bytes 1179656 | tf_op jit(solution)/shard_map/ppermute | solution.py:25
  18.4 0.9 slice.244
  19.3 1.6 copy.26
  21.0 5.5 %collective-permute-done.3 = f32[2,4,48,256]{3,0,2,1:T(2,128)} collective-permute-done((f32[2,4,48,256]{3,0,2,1:T(2,128)}, f32[2,4,48,256]{3,0,2,1:T(2,128)}, u32[]{:S(2)}, u32[]{:S(2)}) %collective-permute-start.3) | collective-permute-done | bytes 393248 | tf_op jit(solution)/shard_map/ppermute | solution.py:25
  26.5 1.5 fusion.34
  28.0 0.3 slice_add_fusion.2
  28.3 0.0 copy-start.7
  28.3 6.3 %scatter-add.15 = f32[4,4,48,256]{3,0,2,1:T(4,128)S(1)} dynamic-update-slice(f32[4,4,48,256]{3,0,2,1:T(4,128)S(1)} %fusion.34, f32[1,4,48,256]{3,0,2,1:T(1,128)S(1)} %slice_add_fusion.2, s32[]{:T(128)} %constant.118.clone.1, s32[]{:T(128)} %constant.118.clone.1, s32[]{:T(128)} %constant.118.clone.1, s32[]{:T(128)} %constant.118.clone.1) | dynamic-update-slice | bytes 393220 | tf_op jit(solution)/shard_map/scatter-add | solution.py:75
  34.6 0.1 convert_bitcast_fusion
  34.8 0.2 pad.19
  34.9 0.1 copy.29
  35.1 1.8 fusion.50
  36.9 0.7 fusion.48
  37.6 0.1 copy.34
  37.6 0.7 reshape.216
  38.3 0.9 slice_bitcast_fusion.4
  39.2 3.8 %collective-permute-start.4 = (bf16[4,1,48,256]{3,2,1,0:T(8,128)(2,1)S(1)}, bf16[4,1,48,256]{3,2,1,0:T(8,128)(2,1)}, u32[]{:S(2)}, u32[]{:S(2)}) collective-permute-start(bf16[4,1,48,256]{3,2,1,0:T(8,128)(2,1)S(1)} %slice_bitcast_fusion.4), channel_id=1, source_target_pairs={{0,2},{2,4},{4,6},{6,8},{8,10},{10,12},{12,14},{1,3},{3,5},{5,7},{... | collective-permute-start | bytes 294920 | tf_op jit(solution)/shard_map/ppermute | solution.py:16
  43.1 1.6 copy.35
  44.7 1.0 reshape.218
  45.7 1.3 collective-permute-start.5
  47.0 0.1 slice.251
  47.1 0.6 copy.30
  47.7 0.1 slice.252
  47.8 0.0 copy-start.4
  47.9 0.1 copy.57
  48.0 0.2 copy.32
  48.3 0.1 slice.254
  48.4 2.6 collective-permute-done.5
  51.0 0.9 fusion.38
  52.0 1.1 fusion.35
  53.1 2.6 collective-permute-start
  55.7 1.3 collective-permute-start.1
  57.0 0.3 collective-permute-done
  57.4 7.5 %collective-permute-done.1 = bf16[4,1,48,256]{3,2,1,0:T(8,128)(2,1)S(1)} collective-permute-done((bf16[4,1,48,256]{3,2,1,0:T(8,128)(2,1)S(1)}, bf16[4,1,48,256]{3,2,1,0:T(8,128)(2,1)S(1)}, u32[]{:S(2)}, u32[]{:S(2)}) %collective-permute-start.1) | collective-permute-done | bytes 98336 | tf_op jit(solution)/shard_map/ppermute | solution.py:17
  64.9 0.1 pad_maximum_fusion.2
  65.0 0.5 copy.41
  65.4 0.0 copy-start.8
  65.5 0.2 pad.17.clone
  65.7 0.1 slice.238
  65.8 0.4 fusion.7
  66.2 1.2 fusion.1
  67.4 0.4 copy.22
  67.8 0.1 slice.239
  68.0 2.1 collective-permute-start.2
  70.1 2.1 fusion.25
  72.3 10.4 %collective-permute-done.2 = bf16[2,4,48,256]{3,2,1,0:T(8,128)(2,1)S(1)} collective-permute-done((bf16[2,4,48,256]{3,2,1,0:T(8,128)(2,1)S(1)}, bf16[2,4,48,256]{3,2,1,0:T(8,128)(2,1)S(1)}, u32[]{:S(2)}, u32[]{:S(2)}) %collective-permute-start.2) | collective-permute-done | bytes 196640 | tf_op jit(solution)/shard_map/ppermute | solution.py:25
  82.7 0.0 copy-start.2
  82.7 0.1 fusion.5
  82.8 0.5 fusion.51
  83.3 0.1 copy-done.2
  83.5 2.0 maximum_multiply_fusion
  85.4 203.2 %all-reduce.2 = bf16[3072,256]{1,0:T(8,128)(2,1)S(1)} all-reduce(f32[3072,256]{1,0:T(8,128)} %maximum_multiply_fusion), channel_id=1, replica_groups=mesh['tm'=32,'height'=8,'dp'=2] {'tm','height','dp'}, use_global_device_ids=true, to_apply=%region_0.1 | all-reduce | flops 786432 | bytes 4718592 | tf_op jit(solution)/shard_map/psum | solution.py:109
  288.6 0.0 copy-start.3
  288.7 0.0 copy-start.5
  288.7 0.8 slice.261
  289.5 1.1 slice.260
  290.5 1.2 fusion.3
  (22 shorter events, 0.3 us)
Async XLA Ops:
  0.6 34.4 %copy-start = (bf16[3,3,256,256]{3,2,1,0:T(8,128)(2,1)S(1)}, bf16[3,3,256,256]{3,2,1,0:T(8,128)(2,1)}, u32[]{:S(2)}) copy-start(bf16[3,3,256,256]{3,2,1,0:T(8,128)(2,1)} %param.14) | copy-start | bytes 3538948
  5.3 21.2 %collective-permute-start.3 = (f32[2,4,48,256]{3,0,2,1:T(2,128)}, f32[2,4,48,256]{3,0,2,1:T(2,128)}, u32[]{:S(2)}, u32[]{:S(2)}) collective-permute-start(f32[2,4,48,256]{3,0,2,1:T(2,128)} %copy.24), channel_id=1, source_target_pairs={{16,0},{32,16},{48,32},{64,48},{80,64},{96,80},{112,96},{128,112},... | collective-permute-start | bytes 1179656 | tf_op jit(solution)/shard_map/ppermute | solution.py:25
  28.3 6.8 %copy-start.7 = (pred[32,7]{0,1:T(8,128)(4,1)S(1)}, pred[32,7]{0,1:T(8,128)(4,1)}, u32[]{:S(2)}) copy-start(pred[32,7]{0,1:T(8,128)(4,1)} %constant.137) | copy-start | bytes 676
  39.2 9.2 %collective-permute-start.4 = (bf16[4,1,48,256]{3,2,1,0:T(8,128)(2,1)S(1)}, bf16[4,1,48,256]{3,2,1,0:T(8,128)(2,1)}, u32[]{:S(2)}, u32[]{:S(2)}) collective-permute-start(bf16[4,1,48,256]{3,2,1,0:T(8,128)(2,1)S(1)} %slice_bitcast_fusion.4), channel_id=1, source_target_pairs={{0,2},{2,4},{4,6},{6,8},{8,10},{10,12},{12,14},{1,3},{3,5},{5,7},{... | collective-permute-start | bytes 294920 | tf_op jit(solution)/shard_map/ppermute | solution.py:16
  45.7 5.4 %collective-permute-start.5 = (bf16[4,1,48,256]{3,2,1,0:T(8,128)(2,1)S(1)}, bf16[4,1,48,256]{3,2,1,0:T(8,128)(2,1)S(1)}, u32[]{:S(2)}, u32[]{:S(2)}) collective-permute-start(bf16[4,1,48,256]{3,2,1,0:T(8,128)(2,1)S(1)} %slice_bitcast_fusion.3), channel_id=1, source_target_pairs={{2,0},{4,2},{6,4},{8,6},{10,8},{12,10},{14,12},{3,1},{5,3},{7,5},{... | collective-permute-start | bytes 294920 | tf_op jit(solution)/shard_map/ppermute | solution.py:17
  47.8 4.2 %copy-start.1 = (bf16[1,4,4,48,256]{4,3,2,1,0:T(8,128)(2,1)S(1)}, bf16[1,4,4,48,256]{4,3,2,1,0:T(8,128)(2,1)}, u32[]{:S(2)}) copy-start(bf16[1,4,4,48,256]{4,3,2,1,0:T(8,128)(2,1)} %param.13) | copy-start | bytes 1179652
  47.8 4.2 %copy-start.4 = (bf16[1,4,4,48,256]{4,3,2,1,0:T(8,128)(2,1)S(1)}, bf16[1,4,4,48,256]{4,3,2,1,0:T(8,128)(2,1)}, u32[]{:S(2)}) copy-start(bf16[1,4,4,48,256]{4,3,2,1,0:T(8,128)(2,1)} %param.12) | copy-start | bytes 1179652
  53.1 4.2 %collective-permute-start = (bf16[4,1,48,256]{3,2,1,0:T(8,128)(2,1)S(1)}, bf16[4,1,48,256]{3,2,1,0:T(8,128)(2,1)S(1)}, u32[]{:S(2)}, u32[]{:S(2)}) collective-permute-start(bf16[4,1,48,256]{3,2,1,0:T(8,128)(2,1)S(1)} %get-tuple-element.66), channel_id=1, source_target_pairs={{0,2},{2,4},{4,6},{6,8},{8,10},{10,12},{12,14},{1,3},{3,5},{5,7},{... | collective-permute-start | bytes 294920 | tf_op jit(solution)/shard_map/ppermute | solution.py:16
  55.7 9.1 %collective-permute-start.1 = (bf16[4,1,48,256]{3,2,1,0:T(8,128)(2,1)S(1)}, bf16[4,1,48,256]{3,2,1,0:T(8,128)(2,1)S(1)}, u32[]{:S(2)}, u32[]{:S(2)}) collective-permute-start(bf16[4,1,48,256]{3,2,1,0:T(8,128)(2,1)S(1)} %get-tuple-element.67), channel_id=1, source_target_pairs={{2,0},{4,2},{6,4},{8,6},{10,8},{12,10},{14,12},{3,1},{5,3},{7,5},{... | collective-permute-start | bytes 294920 | tf_op jit(solution)/shard_map/ppermute | solution.py:17
  65.4 0.7 copy-start.8
  68.0 14.7 %collective-permute-start.2 = (bf16[2,4,48,256]{3,2,1,0:T(8,128)(2,1)S(1)}, bf16[2,4,48,256]{3,2,1,0:T(8,128)(2,1)S(1)}, u32[]{:S(2)}, u32[]{:S(2)}) collective-permute-start(bf16[2,4,48,256]{3,2,1,0:T(8,128)(2,1)S(1)} %slice.241), channel_id=1, source_target_pairs={{0,16},{16,32},{32,48},{48,64},{64,80},{80,96},{96,112},{112,128},... | collective-permute-start | bytes 589832 | tf_op jit(solution)/shard_map/ppermute | solution.py:25
  82.7 0.7 copy-start.2
  288.6 1.9 copy-start.3
  288.7 1.9 copy-start.5
  288.7 1.9 copy-start.6

commit v2 on v0

--- a/solution.py
+++ b/solution.py
@@ -98,14 +98,7 @@
     grad_pad = jnp.pad(frame_grad, ((0, 0), (2, 2), (1, 1), (0, 0)))
     grad_ext = flat_dot(backward_taps(grad_pad, row_count + 2, col_count), spatial_back)
     grad_ext = grad_ext.reshape(frame_count, row_count + 2, col_count, channels)
-    edge_rows = jnp.stack([grad_ext[:, 0], grad_ext[:, row_count + 1]], axis=1)
-    arrived = extended(edge_rows.astype(jnp.bfloat16), (("height", 1),), 1).astype(edge_rows.dtype)
-    act_grad = grad_ext[:, 1 : row_count + 1]
-    act_grad = act_grad.at[:, 0].add(arrived[:, 0])
-    act_grad = act_grad.at[:, row_count - 1].add(arrived[:, 3])
-    input_grad = (
-        upstream.astype(jnp.float32) + silu_slope(inputs.astype(jnp.float32)) * act_grad
-    ).astype(jnp.bfloat16)
+    edge_rows = jnp.stack([grad_ext[:, 0], grad_ext[:, row_count + 1]], axis=1).astype(jnp.bfloat16)
     cell_count = (
         frame_count
         * lax.axis_size("tm")
@@ -123,7 +116,15 @@
         frame_stack, upstream.reshape(-1, channels), contract, preferred_element_type=jnp.float32
     )
     weight_terms = jnp.concatenate([spatial_term, temporal_term], axis=0) * grad_scale
+    weight_terms, edge_rows = lax.optimization_barrier((weight_terms, edge_rows))
     summed = lax.psum(weight_terms, ("tm", "height", "dp")).astype(jnp.bfloat16)
+    arrived = extended(edge_rows, (("height", 1),), 1).astype(jnp.float32)
+    act_grad = grad_ext[:, 1 : row_count + 1]
+    act_grad = act_grad.at[:, 0].add(arrived[:, 0])
+    act_grad = act_grad.at[:, row_count - 1].add(arrived[:, 3])
+    input_grad = (
+        upstream.astype(jnp.float32) + silu_slope(inputs.astype(jnp.float32)) * act_grad
+    ).astype(jnp.bfloat16)
     spatial_grad = summed[: 9 * channels].reshape(3, 3, channels, channels)
     temporal_grad = summed[9 * channels :].reshape(3, channels, channels)
     return (decoded[None], input_grad[None], spatial_grad, temporal_grad)

time: 289 us -> 283 us (0.979)
  waiting for transfers between devices: 22.6 us -> 12.6 us
  other arithmetic: 3.42 us -> 8.83 us
  blocking collectives: 204 us -> 199 us
    ppermute x2, waiting for transfers between devices: 11.3 us -> 0.01 us  [extended(): after = lax.ppermute(initial, axis, down)]
    psum x1, blocking collectives: 204 us -> 199 us  [local(): summed = lax.psum(weight_terms, ('tm', 'height', 'dp')).astype(jnp.bfloat16)]
  transfers between devices with their start and end apart: 6 -> 6, of which waited for: 5 -> 1; matrix products, arithmetic and copies ran while one was open for 6% -> 10% of each run, Pallas kernels for 0% -> 0%
where the time goes in v2:
time: 283 us; the launch traced here: 280 us
  blocking collectives  199 us (70%)
  starting transfers between devices  26.1 us (9%)
  local copies, waits for them, and re-layouts  25.1 us (9%)
  waiting for transfers between devices  12.6 us (4%)
  other arithmetic  8.83 us (3%)
  matrix products  7.21 us (3%)
    psum x1, blocking collectives, local(): summed = lax.psum(weight_terms, ('tm', 'height', 'dp')).astype(jnp.bfloat16)  199 us
    ppermute x2, starting transfers between devices, from_behind(): return lax.ppermute(block, axis, route)  15.3 us
    unnamed x58, local copies, waits for them, and re-layouts  15 us
    ppermute x2, waiting for transfers between devices, from_behind(): return lax.ppermute(block, axis, route)  12.6 us
    ppermute x2, starting transfers between devices, extended(): before = lax.ppermute(last, axis, up)  8.18 us
  transfers between devices with their start and end apart: 6, of which 1 were waited for; matrix products, arithmetic and copies ran while one was open for 10% of the time, Pallas kernels for 0%

profile of v2, /device:TPU:7, one launch (start us, length us, event | category | flops | bytes accessed | tf_op | source)
XLA Modules:
  0.0 279.7 jit_solution(2880313545021962225)
XLA Ops:
  0.6 1.5 pad_slice_fusion.11
  2.2 0.1 pad_maximum_fusion
  2.4 0.7 fusion.42
  3.1 0.0 copy-start
  3.1 0.8 fusion.57
  3.9 13.3 %collective-permute-start.3 = (f32[2,4,48,256]{3,2,1,0:T(8,128)}, f32[2,4,48,256]{3,2,1,0:T(8,128)}, u32[]{:S(2)}, u32[]{:S(2)}) collective-permute-start(f32[2,4,48,256]{3,2,1,0:T(8,128)} %bitcast.21), channel_id=1, source_target_pairs={{16,0},{32,16},{48,32},{64,48},{80,64},{96,80},{112,96},{128,112},... | collective-permute-start | bytes 1179656 | tf_op jit(solution)/shard_map/ppermute | solution.py:25
  17.2 0.2 fusion.22
  17.4 0.7 fusion.59
  18.1 3.8 %collective-permute-start = (bf16[4,1,48,256]{3,2,1,0:T(8,128)(2,1)}, bf16[4,1,48,256]{3,2,1,0:T(8,128)(2,1)}, u32[]{:S(2)}, u32[]{:S(2)}) collective-permute-start(bf16[4,1,48,256]{3,2,1,0:T(8,128)(2,1)} %get-tuple-element.77), channel_id=1, source_target_pairs={{0,2},{2,4},{4,6},{6,8},{8,10},{10,12},{12,14},{1,3},{3,5},{5,7},{... | collective-permute-start | bytes 294920 | tf_op jit(solution)/shard_map/ppermute | solution.py:16
  22.0 1.3 collective-permute-start.1
  23.2 0.7 fusion.51
  24.0 1.0 fusion.56
  25.0 1.0 copy.20
  26.0 0.7 bitcast_dynamic-update-slice_fusion.8
  26.7 1.0 copy.21
  27.7 1.0 copy.22
  28.7 1.0 copy.23
  29.7 1.0 copy.24
  30.7 1.0 copy.25
  31.8 1.0 copy.26
  32.8 1.0 copy.27
  33.8 0.7 bitcast_dynamic-update-slice_fusion.7
  34.4 0.7 bitcast_dynamic-update-slice_fusion.6
  35.1 0.7 bitcast_dynamic-update-slice_fusion.5
  35.8 0.7 bitcast_dynamic-update-slice_fusion.4
  36.4 0.7 bitcast_dynamic-update-slice_fusion.3
  37.1 0.7 bitcast_dynamic-update-slice_fusion.2
  37.7 0.7 bitcast_dynamic-update-slice_fusion.1
  38.4 0.1 copy.28
  38.5 1.2 fusion.29
  39.8 0.9 fusion.41
  40.7 0.1 slice_dynamic-update-slice_fusion.4
  40.9 0.2 constant_dynamic-update-slice_fusion
  41.1 0.1 slice_dynamic-update-slice_fusion.2
  41.3 0.9 fusion.40
  42.2 0.1 slice_dynamic-update-slice_fusion
  42.4 1.1 convolution_convert_fusion
  43.5 2.1 collective-permute-start.2
  45.6 12.6 %collective-permute-done.2 = bf16[2,4,48,256]{3,2,1,0:T(8,128)(2,1)S(1)} collective-permute-done((bf16[2,4,48,256]{3,2,1,0:T(8,128)(2,1)S(1)}, bf16[2,4,48,256]{3,2,1,0:T(8,128)(2,1)S(1)}, u32[]{:S(2)}, u32[]{:S(2)}) %collective-permute-start.2) | collective-permute-done | bytes 196640 | tf_op jit(solution)/shard_map/ppermute | solution.py:25
  58.2 0.1 fusion.39
  58.3 1.2 fusion.2
  59.5 0.5 fusion.8
  60.1 0.6 slice-done
  60.7 1.0 add_dynamic-update-slice_fusion
  61.8 0.1 fusion.30
  62.0 1.1 convolution_bitcast_fusion
  63.1 0.1 fusion.32
  63.3 0.1 fusion.33
  63.5 0.1 fusion.35
  63.6 0.1 fusion.36
  63.8 0.1 fusion.38
  63.9 2.6 fusion.61
  66.6 0.3 maximum_multiply_fusion
  66.9 0.4 copy-done.2
  67.3 0.7 fusion.60
  68.0 4.3 %collective-permute-start.4 = (bf16[4,1,48,256]{3,2,1,0:T(8,128)(2,1)}, bf16[4,1,48,256]{3,2,1,0:T(8,128)(2,1)}, u32[]{:S(2)}, u32[]{:S(2)}) collective-permute-start(bf16[4,1,48,256]{3,2,1,0:T(8,128)(2,1)} %get-tuple-element.79), channel_id=1, source_target_pairs={{0,2},{2,4},{4,6},{6,8},{8,10},{10,12},{12,14},{1,3},{3,5},{5,7},{... | collective-permute-start | bytes 294920 | tf_op jit(solution)/shard_map/ppermute | solution.py:16
  72.3 1.3 collective-permute-start.5
  73.6 198.8 %all-reduce.4 = bf16[3072,256]{1,0:T(8,128)(2,1)} all-reduce(f32[3072,256]{1,0:T(8,128)S(1)} %maximum_multiply_fusion), channel_id=1, replica_groups=mesh['tm'=32,'height'=8,'dp'=2] {'tm','height','dp'}, use_global_device_ids=true, to_apply=%region_0.1 | all-reduce | flops 786432 | bytes 4718592 | tf_op jit(solution)/shard_map/psum | solution.py:120
  272.4 2.5 slice.369
  274.9 1.8 slice.370
  276.7 0.1 slice.364
  276.8 0.9 fusion.50
  277.7 0.9 fusion.49
  278.6 1.1 fusion.48
  (47 shorter events, 0.5 us)
Async XLA Ops:
  0.6 1.6 copy-start.11
  2.4 14.8 %copy-start.1 = (bf16[1,4,4,48,256]{4,3,2,1,0:T(8,128)(2,1)S(1)}, bf16[1,4,4,48,256]{4,3,2,1,0:T(8,128)(2,1)}, u32[]{:S(2)}) copy-start(bf16[1,4,4,48,256]{4,3,2,1,0:T(8,128)(2,1)} %param.12) | copy-start | bytes 1179652
  3.1 35.3 %copy-start = (f32[1152,256]{1,0:T(8,128)}, f32[1152,256]{1,0:T(8,128)S(1)}, u32[]{:S(2)}) copy-start(f32[1152,256]{1,0:T(8,128)S(1)} %fusion.42) | copy-start | bytes 3538948
  3.1 20.9 %copy-start.6 = (bf16[3,3,256,256]{3,2,1,0:T(8,128)(2,1)S(1)}, bf16[3,3,256,256]{3,2,1,0:T(8,128)(2,1)}, u32[]{:S(2)}) copy-start(bf16[3,3,256,256]{3,2,1,0:T(8,128)(2,1)} %param.14) | copy-start | bytes 3538948
  3.9 56.2 %collective-permute-start.3 = (f32[2,4,48,256]{3,2,1,0:T(8,128)}, f32[2,4,48,256]{3,2,1,0:T(8,128)}, u32[]{:S(2)}, u32[]{:S(2)}) collective-permute-start(f32[2,4,48,256]{3,2,1,0:T(8,128)} %bitcast.21), channel_id=1, source_target_pairs={{16,0},{32,16},{48,32},{64,48},{80,64},{96,80},{112,96},{128,112},... | collective-permute-start | bytes 1179656 | tf_op jit(solution)/shard_map/ppermute | solution.py:25
  18.1 20.4 %collective-permute-start = (bf16[4,1,48,256]{3,2,1,0:T(8,128)(2,1)}, bf16[4,1,48,256]{3,2,1,0:T(8,128)(2,1)}, u32[]{:S(2)}, u32[]{:S(2)}) collective-permute-start(bf16[4,1,48,256]{3,2,1,0:T(8,128)(2,1)} %get-tuple-element.77), channel_id=1, source_target_pairs={{0,2},{2,4},{4,6},{6,8},{8,10},{10,12},{12,14},{1,3},{3,5},{5,7},{... | collective-permute-start | bytes 294920 | tf_op jit(solution)/shard_map/ppermute | solution.py:16
  22.0 16.6 %collective-permute-start.1 = (bf16[4,1,48,256]{3,2,1,0:T(8,128)(2,1)}, bf16[4,1,48,256]{3,2,1,0:T(8,128)(2,1)}, u32[]{:S(2)}, u32[]{:S(2)}) collective-permute-start(bf16[4,1,48,256]{3,2,1,0:T(8,128)(2,1)} %get-tuple-element.78), channel_id=1, source_target_pairs={{2,0},{4,2},{6,4},{8,6},{10,8},{12,10},{14,12},{3,1},{5,3},{7,5},{... | collective-permute-start | bytes 294920 | tf_op jit(solution)/shard_map/ppermute | solution.py:17
  28.7 9.7 %copy-start.10 = (bf16[1,1,256,256]{3,2,1,0:T(8,128)(2,1)S(1)}, bf16[1,1,256,256]{3,2,1,0:T(8,128)(2,1)}, u32[]{:S(2)}) copy-start(bf16[1,1,256,256]{3,2,1,0:T(8,128)(2,1)} %get-tuple-element.56) | copy-start | bytes 393220
  40.9 1.5 copy-start.7
  42.4 3.2 %copy-start.13 = (bf16[2304,256]{1,0:T(8,128)(2,1)S(1)}, bf16[2304,256]{1,0:T(8,128)(2,1)}, u32[]{:S(2)}) copy-start(bf16[2304,256]{1,0:T(8,128)(2,1)} %bitcast_dynamic-update-slice_fusion.1) | copy-start | bytes 3538948
  43.5 14.8 %copy-start.12 = (bf16[3,256,256]{2,1,0:T(8,128)(2,1)S(1)}, bf16[3,256,256]{2,1,0:T(8,128)(2,1)}, u32[]{:S(2)}) copy-start(bf16[3,256,256]{2,1,0:T(8,128)(2,1)} %param.15) | copy-start | bytes 1179652
  43.5 14.7 %collective-permute-start.2 = (bf16[2,4,48,256]{3,2,1,0:T(8,128)(2,1)S(1)}, bf16[2,4,48,256]{3,2,1,0:T(8,128)(2,1)S(1)}, u32[]{:S(2)}, u32[]{:S(2)}) collective-permute-start(bf16[2,4,48,256]{3,2,1,0:T(8,128)(2,1)S(1)} %bitcast.117), channel_id=1, source_target_pairs={{0,16},{16,32},{32,48},{48,64},{64,80},{80,96},{96,112},{112,128},... | collective-permute-start | bytes 589832 | tf_op jit(solution)/shard_map/ppermute | solution.py:25
  58.3 1.2 copy-start.4
  59.5 1.1 slice-start
  59.5 2.2 copy-start.9
  66.6 0.7 copy-start.2
  68.0 208.8 %collective-permute-start.4 = (bf16[4,1,48,256]{3,2,1,0:T(8,128)(2,1)}, bf16[4,1,48,256]{3,2,1,0:T(8,128)(2,1)}, u32[]{:S(2)}, u32[]{:S(2)}) collective-permute-start(bf16[4,1,48,256]{3,2,1,0:T(8,128)(2,1)} %get-tuple-element.79), channel_id=1, source_target_pairs={{0,2},{2,4},{4,6},{6,8},{8,10},{10,12},{12,14},{1,3},{3,5},{5,7},{... | collective-permute-start | bytes 294920 | tf_op jit(solution)/shard_map/ppermute | solution.py:16
  72.3 204.4 %collective-permute-start.5 = (bf16[4,1,48,256]{3,2,1,0:T(8,128)(2,1)}, bf16[4,1,48,256]{3,2,1,0:T(8,128)(2,1)}, u32[]{:S(2)}, u32[]{:S(2)}) collective-permute-start(bf16[4,1,48,256]{3,2,1,0:T(8,128)(2,1)} %get-tuple-element.80), channel_id=1, source_target_pairs={{2,0},{4,2},{6,4},{8,6},{10,8},{12,10},{14,12},{3,1},{5,3},{7,5},{... | collective-permute-start | bytes 294920 | tf_op jit(solution)/shard_map/ppermute | solution.py:17
  272.4 4.3 %copy-start.8 = (f32[4,6,48,256]{3,2,1,0:T(8,128)S(1)}, f32[4,6,48,256]{3,2,1,0:T(8,128)}, u32[]{:S(2)}) copy-start(f32[4,6,48,256]{3,2,1,0:T(8,128)} %get-tuple-element.82) | copy-start | bytes 3538948
  272.4 4.4 %copy-start.3 = (bf16[4,2,48,256]{3,2,1,0:T(8,128)(2,1)S(1)}, bf16[4,2,48,256]{3,2,1,0:T(8,128)(2,1)}, u32[]{:S(2)}) copy-start(bf16[4,2,48,256]{3,2,1,0:T(8,128)(2,1)} %copy-done.2) | copy-start | bytes 589828
  274.9 3.8 %copy-start.5 = (bf16[1,4,4,48,256]{4,3,2,1,0:T(8,128)(2,1)S(1)}, bf16[1,4,4,48,256]{4,3,2,1,0:T(8,128)(2,1)}, u32[]{:S(2)}) copy-start(bf16[1,4,4,48,256]{4,3,2,1,0:T(8,128)(2,1)} %param.13) | copy-start | bytes 1179652

commit v3 on v0

--- a/solution.py
+++ b/solution.py
@@ -71,41 +71,51 @@
     )
     temporal_back = jnp.concatenate([w_temporal[2].T, w_temporal[1].T, w_temporal[0].T], axis=0)
     first_shard = lax.axis_index("tm") == 0
-    activated = jax.nn.silu(inputs.astype(jnp.float32)).astype(jnp.bfloat16)
-    activ_rows = extended(activated, (("height", 1),), 1)
-    activ_pad = jnp.pad(activ_rows, ((0, 0), (0, 0), (1, 1), (0, 0)))
-    activ_taps = forward_taps(activ_pad, row_count, col_count).reshape(-1, 9 * channels)
-    spatial_out = jnp.dot(activ_taps, spatial_flat, preferred_element_type=jnp.float32)
-    spatial_out = spatial_out.astype(jnp.bfloat16).reshape(inputs.shape)
-    earlier = from_behind(spatial_out[frame_count - 2 :], "tm", 1)
-    repeated = jnp.broadcast_to(spatial_out[:1], earlier.shape)
-    earlier = jnp.where(first_shard, repeated, earlier)
+    inputs_prev = from_behind(inputs[frame_count - 2 :], "tm", 1)
+    upstream_next = from_behind(upstream[:2], "tm", -1)
+    both = jnp.concatenate(
+        [
+            jnp.concatenate([inputs_prev, inputs], axis=0),
+            jnp.concatenate([upstream, upstream_next], axis=0),
+        ],
+        axis=-1,
+    )
+    both = extended(both, (("height", 1),), 1)
+    inputs_full = both[..., :channels]
+    upstream_full = both[..., channels:]
+    activated = jax.nn.silu(inputs_full.astype(jnp.float32)).astype(jnp.bfloat16)
+    activ_pad = jnp.pad(activated, ((0, 0), (0, 0), (1, 1), (0, 0)))
+    activ_taps = forward_taps(activ_pad, row_count, col_count)
+    spatial_all = flat_dot(activ_taps, spatial_flat).astype(jnp.bfloat16)
+    spatial_all = spatial_all.reshape(frame_count + 2, row_count, col_count, channels)
+    spatial_out = spatial_all[2:]
+    repeated = jnp.broadcast_to(spatial_out[:1], (2,) + spatial_out.shape[1:])
+    earlier = jnp.where(first_shard, repeated, spatial_all[:2])
     padded_frames = jnp.concatenate([earlier, spatial_out], axis=0)
     frame_stack = frame_taps(padded_frames, frame_count).reshape(-1, 3 * channels)
     temporal_out = jnp.dot(frame_stack, temporal_flat, preferred_element_type=jnp.float32).reshape(
         inputs.shape
     )
     decoded = (inputs.astype(jnp.float32) + temporal_out).astype(jnp.bfloat16)
-    upstream_ext = jnp.pad(upstream, ((2, 2), (0, 0), (0, 0), (0, 0)))
-    frame_part = flat_dot(frame_taps(upstream_ext, frame_count + 2), temporal_back)
-    frame_part = frame_part.reshape(frame_count + 2, row_count, col_count, channels)
-    rim_part = frame_part[:2]
-    returned = from_behind(rim_part, "tm", -1)
-    frame_sum = frame_part[2:]
-    frame_sum = frame_sum.at[frame_count - 2 :].add(returned)
-    frame_sum = frame_sum.at[0].add(jnp.where(first_shard, rim_part[0] + rim_part[1], 0.0))
-    frame_grad = frame_sum.astype(jnp.bfloat16)
-    grad_pad = jnp.pad(frame_grad, ((0, 0), (2, 2), (1, 1), (0, 0)))
-    grad_ext = flat_dot(backward_taps(grad_pad, row_count + 2, col_count), spatial_back)
-    grad_ext = grad_ext.reshape(frame_count, row_count + 2, col_count, channels)
-    edge_rows = jnp.stack([grad_ext[:, 0], grad_ext[:, row_count + 1]], axis=1)
-    arrived = extended(edge_rows.astype(jnp.bfloat16), (("height", 1),), 1).astype(edge_rows.dtype)
-    act_grad = grad_ext[:, 1 : row_count + 1]
-    act_grad = act_grad.at[:, 0].add(arrived[:, 0])
-    act_grad = act_grad.at[:, row_count - 1].add(arrived[:, 3])
+    frame_sum = flat_dot(frame_taps(upstream_full, frame_count), temporal_back)
+    first_up = upstream_full[0].reshape(-1, channels)
+    second_up = upstream_full[1].reshape(-1, channels)
+    fold_term = jnp.dot(first_up, w_temporal[0].T, preferred_element_type=jnp.float32)
+    fold_term = fold_term + jnp.dot(first_up, w_temporal[1].T, preferred_element_type=jnp.float32)
+    fold_term = fold_term + jnp.dot(second_up, w_temporal[0].T, preferred_element_type=jnp.float32)
+    fold_rows = frame_sum.shape[0] // frame_count
+    frame_sum = frame_sum.reshape(frame_count, fold_rows, channels)
+    frame_sum = frame_sum.at[0].add(jnp.where(first_shard, fold_term, 0.0))
+    frame_grad_full = frame_sum.astype(jnp.bfloat16).reshape(
+        frame_count, row_count + 2, col_count, channels
+    )
+    grad_pad = jnp.pad(frame_grad_full, ((0, 0), (0, 0), (1, 1), (0, 0)))
+    act_grad = flat_dot(backward_taps(grad_pad, row_count, col_count), spatial_back)
+    act_grad = act_grad.reshape(inputs.shape)
     input_grad = (
         upstream.astype(jnp.float32) + silu_slope(inputs.astype(jnp.float32)) * act_grad
     ).astype(jnp.bfloat16)
+    frame_grad = frame_grad_full[:, 1 : row_count + 1]
     cell_count = (
         frame_count
         * lax.axis_size("tm")
@@ -116,8 +126,9 @@
     )
     grad_scale = 1.0 / math.sqrt(cell_count)
     contract = (((0,), (0,)), ((), ()))
+    local_taps = activ_taps[2:].reshape(-1, 9 * channels)
     spatial_term = lax.dot_general(
-        activ_taps, frame_grad.reshape(-1, channels), contract, preferred_element_type=jnp.float32
+        local_taps, frame_grad.reshape(-1, channels), contract, preferred_element_type=jnp.float32
     )
     temporal_term = lax.dot_general(
         frame_stack, upstream.reshape(-1, channels), contract, preferred_element_type=jnp.float32

time: 289 us -> 276 us (0.955)
  waiting for transfers between devices: 22.6 us -> 14.3 us
  starting transfers between devices: 24.2 us -> 19.6 us
  local copies, waits for them, and re-layouts: 25.6 us -> 22.1 us
    ppermute x2 -> x1, waiting for transfers between devices: 11.3 us -> 3.51 us  [extended(): after = lax.ppermute(initial, axis, down)]
    ppermute x2 -> x1, starting transfers between devices: 6.54 us -> 3.22 us  [extended(): before = lax.ppermute(last, axis, up)]
    unnamed x58 -> x68, local copies, waits for them, and re-layouts: 16.9 us -> 15.1 us
  transfers between devices with their start and end apart: 6 -> 4, of which waited for: 5 -> 2; matrix products, arithmetic and copies ran while one was open for 6% -> 2% of each run, Pallas kernels for 0% -> 0%
where the time goes in v3:
time: 276 us; the launch traced here: 274 us
  blocking collectives  206 us (75%)
  local copies, waits for them, and re-layouts  22.1 us (8%)
  starting transfers between devices  19.6 us (7%)
  waiting for transfers between devices  14.3 us (5%)
  matrix products  7.67 us (3%)
  other arithmetic  3.09 us (1%)
    psum x1, blocking collectives, local(): summed = lax.psum(weight_terms, ('tm', 'height', 'dp')).astype(jnp.bfloat16)  206 us
    unnamed x68, local copies, waits for them, and re-layouts  15.1 us
    ppermute x2, starting transfers between devices, from_behind(): return lax.ppermute(block, axis, route)  15.1 us
    ppermute x2, waiting for transfers between devices, from_behind(): return lax.ppermute(block, axis, route)  10.7 us
  transfers between devices with their start and end apart: 4, of which 2 were waited for; matrix products, arithmetic and copies ran while one was open for 2% of the time, Pallas kernels for 0%

profile of v3, /device:TPU:7, one launch (start us, length us, event | category | flops | bytes accessed | tf_op | source)
XLA Modules:
  0.0 274.2 jit_solution(1824427597816013728)
XLA Ops:
  0.6 1.0 slice_bitcast_fusion
  1.7 13.1 %collective-permute-start.1 = (bf16[2,4,48,256]{3,2,1,0:T(8,128)(2,1)S(1)}, bf16[2,4,48,256]{3,2,1,0:T(8,128)(2,1)S(1)}, u32[]{:S(2)}, u32[]{:S(2)}) collective-permute-start(bf16[2,4,48,256]{3,2,1,0:T(8,128)(2,1)S(1)} %slice_bitcast_fusion), channel_id=1, source_target_pairs={{16,0},{32,16},{48,32},{64,48},{80,64},{96,80},{112,96},{128,112},... | collective-permute-start | bytes 589832 | tf_op jit(solution)/shard_map/ppermute | solution.py:25
  14.8 0.9 slice_bitcast_fusion.1
  15.8 1.9 collective-permute-start
  17.7 1.1 fusion.64
  18.8 0.1 fusion.63
  18.9 0.1 copy.33
  19.0 0.1 copy.32
  19.1 0.1 copy.31
  19.2 0.1 copy.30
  19.3 0.1 copy.29
  19.4 0.1 copy.28
  19.5 0.1 copy.27
  19.6 0.1 copy.26
  19.9 10.7 %collective-permute-done = bf16[2,4,48,256]{3,2,1,0:T(8,128)(2,1)S(1)} collective-permute-done((bf16[2,4,48,256]{3,2,1,0:T(8,128)(2,1)S(1)}, bf16[2,4,48,256]{3,2,1,0:T(8,128)(2,1)S(1)}, u32[]{:S(2)}, u32[]{:S(2)}) %collective-permute-start) | collective-permute-done | bytes 196640 | tf_op jit(solution)/shard_map/ppermute | solution.py:25
  30.6 0.1 maximum_maximum_fusion
  30.7 3.2 %collective-permute-start.2 = (bf16[6,1,48,512]{3,2,1,0:T(8,128)(2,1)S(1)}, bf16[6,1,48,512]{3,2,1,0:T(8,128)(2,1)S(1)}, u32[]{:S(2)}, u32[]{:S(2)}) collective-permute-start(bf16[6,1,48,512]{3,2,1,0:T(8,128)(2,1)S(1)} %get-tuple-element.30), channel_id=1, source_target_pairs={{0,2},{2,4},{4,6},{6,8},{8,10},{10,12},{12,14},{1,3},{3,5},{5,7},{... | collective-permute-start | bytes 884744 | tf_op jit(solution)/shard_map/ppermute | solution.py:16
  33.9 1.3 collective-permute-start.3
  35.2 1.0 copy-done.14
  36.3 0.1 copy.23
  36.4 0.8 copy.24
  37.1 0.8 copy.25
  37.9 0.1 copy.34
  38.0 0.7 bitcast_dynamic-update-slice_fusion
  38.7 3.5 %collective-permute-done.3 = bf16[6,1,48,512]{3,2,1,0:T(8,128)(2,1)S(1)} collective-permute-done((bf16[6,1,48,512]{3,2,1,0:T(8,128)(2,1)S(1)}, bf16[6,1,48,512]{3,2,1,0:T(8,128)(2,1)S(1)}, u32[]{:S(2)}, u32[]{:S(2)}) %collective-permute-start.3) | collective-permute-done | bytes 294944 | tf_op jit(solution)/shard_map/ppermute | solution.py:17
  42.2 0.2 pad_maximum_fusion
  42.4 0.5 fusion.3
  43.0 0.2 fusion.62
  43.1 0.2 fusion.31
  43.3 0.2 fusion.32
  43.6 0.3 fusion.33
  43.9 0.2 fusion.34
  44.2 0.3 fusion.35
  44.5 0.2 fusion.36
  44.7 0.7 copy-done.5
  45.4 1.5 convolution_convert_fusion
  47.1 1.1 copy-done.2
  48.2 0.2 fusion.53
  48.4 0.2 fusion.51
  48.7 0.1 pad_maximum_fusion.1
  48.8 0.6 fusion.44
  49.5 0.3 fusion.25
  49.7 0.1 convert_element_type.38
  49.8 0.9 fusion.37
  50.7 1.1 convolution_bitcast_fusion
  51.9 0.1 fusion.43
  51.9 0.5 fusion.14
  52.5 0.2 copy-done.7
  52.7 0.1 copy-done.9
  52.8 2.0 maximum_multiply_fusion
  54.8 206.3 %all-reduce.3 = bf16[3072,256]{1,0:T(8,128)(2,1)S(1)} all-reduce(f32[3072,256]{1,0:T(8,128)} %maximum_multiply_fusion), channel_id=1, replica_groups=mesh['tm'=32,'height'=8,'dp'=2] {'tm','height','dp'}, use_global_device_ids=true, to_apply=%region_0.1 | all-reduce | flops 786432 | bytes 4718592 | tf_op jit(solution)/shard_map/psum | solution.py:137
  261.1 0.8 slice.266
  261.9 1.1 slice.265
  263.0 0.8 slice_dynamic-update-slice_fusion.4
  263.8 1.0 fusion.38
  264.8 0.9 fusion.39
  265.7 0.8 slice_dynamic-update-slice_fusion.5
  266.5 0.9 fusion.40
  267.4 0.9 fusion.41
  268.3 0.8 slice_dynamic-update-slice_fusion.3
  269.1 0.9 fusion.42
  270.1 1.2 fusion.7
  271.3 1.0 copy-done.13
  272.3 1.9 fusion.8
  (46 shorter events, 0.4 us)
Async XLA Ops:
  0.6 18.1 %copy-start.4 = (bf16[3,3,256,256]{3,2,1,0:T(8,128)(2,1)S(1)}, bf16[3,3,256,256]{3,2,1,0:T(8,128)(2,1)}, u32[]{:S(2)}) copy-start(bf16[3,3,256,256]{3,2,1,0:T(8,128)(2,1)} %param.8) | copy-start | bytes 3538948
  1.7 18.2 %collective-permute-start.1 = (bf16[2,4,48,256]{3,2,1,0:T(8,128)(2,1)S(1)}, bf16[2,4,48,256]{3,2,1,0:T(8,128)(2,1)S(1)}, u32[]{:S(2)}, u32[]{:S(2)}) collective-permute-start(bf16[2,4,48,256]{3,2,1,0:T(8,128)(2,1)S(1)} %slice_bitcast_fusion), channel_id=1, source_target_pairs={{16,0},{32,16},{48,32},{64,48},{80,64},{96,80},{112,96},{128,112},... | collective-permute-start | bytes 589832 | tf_op jit(solution)/shard_map/ppermute | solution.py:25
  15.8 14.8 %collective-permute-start = (bf16[2,4,48,256]{3,2,1,0:T(8,128)(2,1)S(1)}, bf16[2,4,48,256]{3,2,1,0:T(8,128)(2,1)S(1)}, u32[]{:S(2)}, u32[]{:S(2)}) collective-permute-start(bf16[2,4,48,256]{3,2,1,0:T(8,128)(2,1)S(1)} %slice_bitcast_fusion.1), channel_id=1, source_target_pairs={{0,16},{16,32},{32,48},{48,64},{64,80},{80,96},{96,112},{112,128},... | collective-permute-start | bytes 589832 | tf_op jit(solution)/shard_map/ppermute | solution.py:25
  18.9 11.8 %copy-start = (bf16[1,4,4,48,256]{4,3,2,1,0:T(8,128)(2,1)S(1)}, bf16[1,4,4,48,256]{4,3,2,1,0:T(8,128)(2,1)}, u32[]{:S(2)}) copy-start(bf16[1,4,4,48,256]{4,3,2,1,0:T(8,128)(2,1)} %param.7) | copy-start | bytes 1179652
  18.9 11.7 %copy-start.1 = (bf16[1,4,4,48,256]{4,3,2,1,0:T(8,128)(2,1)S(1)}, bf16[1,4,4,48,256]{4,3,2,1,0:T(8,128)(2,1)}, u32[]{:S(2)}) copy-start(bf16[1,4,4,48,256]{4,3,2,1,0:T(8,128)(2,1)} %param.6) | copy-start | bytes 1179652
  30.7 8.0 %collective-permute-start.2 = (bf16[6,1,48,512]{3,2,1,0:T(8,128)(2,1)S(1)}, bf16[6,1,48,512]{3,2,1,0:T(8,128)(2,1)S(1)}, u32[]{:S(2)}, u32[]{:S(2)}) collective-permute-start(bf16[6,1,48,512]{3,2,1,0:T(8,128)(2,1)S(1)} %get-tuple-element.30), channel_id=1, source_target_pairs={{0,2},{2,4},{4,6},{6,8},{8,10},{10,12},{12,14},{1,3},{3,5},{5,7},{... | collective-permute-start | bytes 884744 | tf_op jit(solution)/shard_map/ppermute | solution.py:16
  33.9 8.3 %collective-permute-start.3 = (bf16[6,1,48,512]{3,2,1,0:T(8,128)(2,1)S(1)}, bf16[6,1,48,512]{3,2,1,0:T(8,128)(2,1)S(1)}, u32[]{:S(2)}, u32[]{:S(2)}) collective-permute-start(bf16[6,1,48,512]{3,2,1,0:T(8,128)(2,1)S(1)} %get-tuple-element.31), channel_id=1, source_target_pairs={{2,0},{4,2},{6,4},{8,6},{10,8},{12,10},{14,12},{3,1},{5,3},{7,5},{... | collective-permute-start | bytes 884744 | tf_op jit(solution)/shard_map/ppermute | solution.py:17
  35.2 1.0 copy-start.14
  44.2 1.3 copy-start.5
  47.0 1.8 copy-start.6
  47.0 1.2 copy-start.2
  47.1 1.7 copy-start.11
  47.1 1.7 copy-start.12
  50.7 1.1 slice-start
  50.7 1.1 slice-start.1
  51.9 0.7 copy-start.7
  51.9 0.9 copy-start.9
  265.6 4.4 %copy-start.3 = (bf16[3,256,256]{2,1,0:T(8,128)(2,1)S(1)}, bf16[3,256,256]{2,1,0:T(8,128)(2,1)}, u32[]{:S(2)}) copy-start(bf16[3,256,256]{2,1,0:T(8,128)(2,1)} %param.9) | copy-start | bytes 1179652
  265.6 4.4 %copy-start.8 = (bf16[4,4,48,256]{3,2,1,0:T(8,128)(2,1)S(1)}, bf16[4,4,48,256]{3,2,1,0:T(8,128)(2,1)}, u32[]{:S(2)}) copy-start(bf16[4,4,48,256]{3,2,1,0:T(8,128)(2,1)} %copy-done.7) | copy-start | bytes 1179652
  265.7 4.4 %copy-start.10 = (bf16[4,4,48,256]{3,2,1,0:T(8,128)(2,1)S(1)}, bf16[4,4,48,256]{3,2,1,0:T(8,128)(2,1)}, u32[]{:S(2)}) copy-start(bf16[4,4,48,256]{3,2,1,0:T(8,128)(2,1)} %copy-done.9) | copy-start | bytes 1179652
  269.1 2.1 copy-start.15
  270.0 2.2 copy-start.13

commit v4 on v3

--- a/solution.py
+++ b/solution.py
@@ -73,49 +73,50 @@
     first_shard = lax.axis_index("tm") == 0
     inputs_prev = from_behind(inputs[frame_count - 2 :], "tm", 1)
     upstream_next = from_behind(upstream[:2], "tm", -1)
-    both = jnp.concatenate(
-        [
-            jnp.concatenate([inputs_prev, inputs], axis=0),
-            jnp.concatenate([upstream, upstream_next], axis=0),
-        ],
-        axis=-1,
+    local_both = extended(jnp.concatenate([inputs, upstream], axis=-1), (("height", 1),), 1)
+    rim_both = extended(
+        jnp.concatenate([inputs_prev, upstream_next], axis=-1), (("height", 1),), 1
     )
-    both = extended(both, (("height", 1),), 1)
-    inputs_full = both[..., :channels]
-    upstream_full = both[..., channels:]
-    activated = jax.nn.silu(inputs_full.astype(jnp.float32)).astype(jnp.bfloat16)
-    activ_pad = jnp.pad(activated, ((0, 0), (0, 0), (1, 1), (0, 0)))
-    activ_taps = forward_taps(activ_pad, row_count, col_count)
-    spatial_all = flat_dot(activ_taps, spatial_flat).astype(jnp.bfloat16)
-    spatial_all = spatial_all.reshape(frame_count + 2, row_count, col_count, channels)
-    spatial_out = spatial_all[2:]
+
+    def spatial_forward(block):
+        activ = jax.nn.silu(block.astype(jnp.float32)).astype(jnp.bfloat16)
+        taps = forward_taps(jnp.pad(activ, ((0, 0), (0, 0), (1, 1), (0, 0))), row_count, col_count)
+        out = flat_dot(taps, spatial_flat).astype(jnp.bfloat16)
+        return taps, out.reshape(block.shape[0], row_count, col_count, channels)
+
+    activ_taps, spatial_out = spatial_forward(local_both[..., :channels])
+    unused, spatial_rim = spatial_forward(rim_both[..., :channels])
     repeated = jnp.broadcast_to(spatial_out[:1], (2,) + spatial_out.shape[1:])
-    earlier = jnp.where(first_shard, repeated, spatial_all[:2])
+    earlier = jnp.where(first_shard, repeated, spatial_rim)
     padded_frames = jnp.concatenate([earlier, spatial_out], axis=0)
     frame_stack = frame_taps(padded_frames, frame_count).reshape(-1, 3 * channels)
     temporal_out = jnp.dot(frame_stack, temporal_flat, preferred_element_type=jnp.float32).reshape(
         inputs.shape
     )
     decoded = (inputs.astype(jnp.float32) + temporal_out).astype(jnp.bfloat16)
-    frame_sum = flat_dot(frame_taps(upstream_full, frame_count), temporal_back)
-    first_up = upstream_full[0].reshape(-1, channels)
-    second_up = upstream_full[1].reshape(-1, channels)
-    fold_term = jnp.dot(first_up, w_temporal[0].T, preferred_element_type=jnp.float32)
-    fold_term = fold_term + jnp.dot(first_up, w_temporal[1].T, preferred_element_type=jnp.float32)
-    fold_term = fold_term + jnp.dot(second_up, w_temporal[0].T, preferred_element_type=jnp.float32)
-    fold_rows = frame_sum.shape[0] // frame_count
-    frame_sum = frame_sum.reshape(frame_count, fold_rows, channels)
-    frame_sum = frame_sum.at[0].add(jnp.where(first_shard, fold_term, 0.0))
-    frame_grad_full = frame_sum.astype(jnp.bfloat16).reshape(
-        frame_count, row_count + 2, col_count, channels
-    )
+
+    def frame_gradient(source):
+        rows = source.shape[1]
+        part = flat_dot(frame_taps(source, frame_count), temporal_back)
+        first_up = source[0].reshape(-1, channels)
+        second_up = source[1].reshape(-1, channels)
+        fold = jnp.dot(first_up, w_temporal[0].T, preferred_element_type=jnp.float32)
+        fold = fold + jnp.dot(first_up, w_temporal[1].T, preferred_element_type=jnp.float32)
+        fold = fold + jnp.dot(second_up, w_temporal[0].T, preferred_element_type=jnp.float32)
+        part = part.reshape(frame_count, rows * col_count, channels)
+        part = part.at[0].add(jnp.where(first_shard, fold, 0.0))
+        return part.astype(jnp.bfloat16).reshape(frame_count, rows, col_count, channels)
+
+    frame_grad = frame_gradient(jnp.concatenate([upstream, upstream_next], axis=0))
+    up_rows = jnp.concatenate([local_both[..., channels:], rim_both[..., channels:]], axis=0)
+    edge_grad = frame_gradient(jnp.stack([up_rows[:, 0], up_rows[:, row_count + 1]], axis=1))
+    frame_grad_full = jnp.concatenate([edge_grad[:, :1], frame_grad, edge_grad[:, 1:]], axis=1)
     grad_pad = jnp.pad(frame_grad_full, ((0, 0), (0, 0), (1, 1), (0, 0)))
     act_grad = flat_dot(backward_taps(grad_pad, row_count, col_count), spatial_back)
     act_grad = act_grad.reshape(inputs.shape)
     input_grad = (
         upstream.astype(jnp.float32) + silu_slope(inputs.astype(jnp.float32)) * act_grad
     ).astype(jnp.bfloat16)
-    frame_grad = frame_grad_full[:, 1 : row_count + 1]
     cell_count = (
         frame_count
         * lax.axis_size("tm")
@@ -126,7 +127,7 @@
     )
     grad_scale = 1.0 / math.sqrt(cell_count)
     contract = (((0,), (0,)), ((), ()))
-    local_taps = activ_taps[2:].reshape(-1, 9 * channels)
+    local_taps = activ_taps.reshape(-1, 9 * channels)
     spatial_term = lax.dot_general(
         local_taps, frame_grad.reshape(-1, channels), contract, preferred_element_type=jnp.float32
     )

time: 276 us -> 268 us (0.971)
  waiting for transfers between devices: 14.3 us -> 1.1 us
  starting transfers between devices: 19.6 us -> 24.8 us
  local copies, waits for them, and re-layouts: 22.1 us -> 18.7 us
    ppermute x2, waiting for transfers between devices: 10.7 us -> 1.09 us  [from_behind(): return lax.ppermute(block, axis, route)]
    unnamed x68 -> x101, local copies, waits for them, and re-layouts: 15.1 us -> 9.24 us
    ppermute x1 -> x2, starting transfers between devices: 3.22 us -> 7.08 us  [extended(): before = lax.ppermute(last, axis, up)]
    ppermute x1 -> x2, waiting for transfers between devices: 3.51 us -> 0.01 us  [extended(): after = lax.ppermute(initial, axis, down)]
  transfers between devices with their start and end apart: 4 -> 6, of which waited for: 2 -> 1; matrix products, arithmetic and copies ran while one was open for 2% -> 5% of each run, Pallas kernels for 0% -> 0%
where the time goes in v4:
time: 268 us; the launch traced here: 267 us
  blocking collectives  207 us (77%)
  starting transfers between devices  24.8 us (9%)
  local copies, waits for them, and re-layouts  18.7 us (7%)
  matrix products  8.57 us (3%)
  other arithmetic  4.44 us (2%)
    psum x1, blocking collectives, local(): summed = lax.psum(weight_terms, ('tm', 'height', 'dp')).astype(jnp.bfloat16)  207 us
    ppermute x2, starting transfers between devices, from_behind(): return lax.ppermute(block, axis, route)  15.2 us
    unnamed x101, local copies, waits for them, and re-layouts  9.24 us
    ppermute x2, starting transfers between devices, extended(): before = lax.ppermute(last, axis, up)  7.08 us
  transfers between devices with their start and end apart: 6, of which 1 were waited for; matrix products, arithmetic and copies ran while one was open for 5% of the time, Pallas kernels for 0%

profile of v4, /device:TPU:7, one launch (start us, length us, event | category | flops | bytes accessed | tf_op | source)
XLA Modules:
  0.0 266.5 jit_solution(15410041933886744531)
XLA Ops:
  0.7 1.0 slice_bitcast_fusion
  1.7 13.1 %collective-permute-start.3 = (bf16[2,4,48,256]{3,2,1,0:T(8,128)(2,1)S(1)}, bf16[2,4,48,256]{3,2,1,0:T(8,128)(2,1)S(1)}, u32[]{:S(2)}, u32[]{:S(2)}) collective-permute-start(bf16[2,4,48,256]{3,2,1,0:T(8,128)(2,1)S(1)} %slice_bitcast_fusion), channel_id=1, source_target_pairs={{16,0},{32,16},{48,32},{64,48},{80,64},{96,80},{112,96},{128,112},... | collective-permute-start | bytes 589832 | tf_op jit(solution)/shard_map/ppermute | solution.py:25
  14.8 1.6 slice_bitcast_fusion.1
  16.4 2.0 collective-permute-start.2
  18.5 1.8 pad_maximum_fusion.8
  20.3 3.9 %collective-permute-start = (bf16[4,1,48,512]{3,2,1,0:T(8,128)(2,1)}, bf16[4,1,48,512]{3,2,1,0:T(8,128)(2,1)}, u32[]{:S(2)}, u32[]{:S(2)}) collective-permute-start(bf16[4,1,48,512]{3,2,1,0:T(8,128)(2,1)} %get-tuple-element.37), channel_id=1, source_target_pairs={{0,2},{2,4},{4,6},{6,8},{8,10},{10,12},{12,14},{1,3},{3,5},{5,7},{... | collective-permute-start | bytes 589832 | tf_op jit(solution)/shard_map/ppermute | solution.py:16
  24.2 1.3 collective-permute-start.1
  25.6 0.2 fusion.76
  25.8 0.2 convolution_add_fusion.2
  26.3 0.1 copy.31
  26.4 0.1 copy.30
  26.8 0.1 copy.26
  26.9 0.1 copy.25
  27.2 1.0 copy-done.27
  28.2 0.8 copy.22
  29.0 0.8 copy.23
  29.8 0.8 copy.24
  30.5 1.1 collective-permute-done.2
  31.7 3.2 %collective-permute-start.4 = (bf16[2,1,48,512]{3,2,1,0:T(8,128)(2,1)S(1)}, bf16[2,1,48,512]{3,2,1,0:T(8,128)(2,1)S(1)}, u32[]{:S(2)}, u32[]{:S(2)}) collective-permute-start(bf16[2,1,48,512]{3,2,1,0:T(8,128)(2,1)S(1)} %get-tuple-element.48), channel_id=1, source_target_pairs={{0,2},{2,4},{4,6},{6,8},{8,10},{10,12},{12,14},{1,3},{3,5},{5,7},{... | collective-permute-start | bytes 294920 | tf_op jit(solution)/shard_map/ppermute | solution.py:16
  34.9 1.3 collective-permute-start.5
  36.3 0.5 fusion.15
  36.8 0.2 fusion.72
  37.1 0.7 copy-done.5
  37.8 1.1 pad_maximum_fusion
  38.9 0.4 fusion.9
  39.3 0.1 fusion.52
  39.5 0.1 fusion.53
  39.6 0.1 fusion.54
  39.7 0.1 fusion.55
  39.8 0.1 fusion.56
  40.0 0.1 fusion.57
  40.1 1.1 fusion.100
  41.3 0.1 copy-done.8
  41.4 1.1 convolution_convert_fusion
  42.6 0.2 fusion.47
  42.8 0.4 copy-done.12
  43.2 0.5 slice-done
  43.7 0.6 fusion.97
  44.4 0.8 fusion.98
  45.7 0.6 convolution_convert_fusion.1
  46.3 0.2 slice-done.1
  46.6 0.2 copy-done.13
  46.8 0.7 copy-done.16
  47.5 0.1 copy-done.18
  47.6 0.5 fusion.21
  48.2 0.3 maximum_multiply_fusion
  48.4 207.4 %all-reduce.4 = bf16[3072,256]{1,0:T(8,128)(2,1)} all-reduce(f32[3072,256]{1,0:T(8,128)S(1)} %maximum_multiply_fusion), channel_id=1, replica_groups=mesh['tm'=32,'height'=8,'dp'=2] {'tm','height','dp'}, use_global_device_ids=true, to_apply=%region_0.1 | all-reduce | flops 786432 | bytes 4718592 | tf_op jit(solution)/shard_map/psum | solution.py:138
  255.8 1.9 slice.372
  257.7 2.4 slice.371
  260.1 0.2 fusion.79
  260.2 0.2 convolution_add_fusion.4
  260.6 0.3 fusion.65
  260.9 0.2 fusion.33
  261.2 0.3 fusion.43
  261.5 0.1 slice_dynamic-update-slice_fusion.5
  261.7 0.1 slice_dynamic-update-slice_fusion.3
  261.9 0.1 slice_dynamic-update-slice_fusion.1
  262.1 0.7 copy-done.6
  262.8 0.1 copy-done.14
  263.0 0.1 copy-done.17
  263.1 0.1 copy-done.19
  263.2 1.2 fusion.4
  264.4 0.2 copy-done.28
  264.6 1.9 fusion.5
  (101 shorter events, 1.8 us)
Async XLA Ops:
  0.6 24.8 %copy-start = (bf16[1,4,4,48,256]{4,3,2,1,0:T(8,128)(2,1)S(1)}, bf16[1,4,4,48,256]{4,3,2,1,0:T(8,128)(2,1)}, u32[]{:S(2)}) copy-start(bf16[1,4,4,48,256]{4,3,2,1,0:T(8,128)(2,1)} %param.9) | copy-start | bytes 1179652
  0.6 24.9 %copy-start.3 = (bf16[3,256,256]{2,1,0:T(8,128)(2,1)S(1)}, bf16[3,256,256]{2,1,0:T(8,128)(2,1)}, u32[]{:S(2)}) copy-start(bf16[3,256,256]{2,1,0:T(8,128)(2,1)} %param.11) | copy-start | bytes 1179652
  1.7 30.0 %collective-permute-start.3 = (bf16[2,4,48,256]{3,2,1,0:T(8,128)(2,1)S(1)}, bf16[2,4,48,256]{3,2,1,0:T(8,128)(2,1)S(1)}, u32[]{:S(2)}, u32[]{:S(2)}) collective-permute-start(bf16[2,4,48,256]{3,2,1,0:T(8,128)(2,1)S(1)} %slice_bitcast_fusion), channel_id=1, source_target_pairs={{16,0},{32,16},{48,32},{64,48},{80,64},{96,80},{112,96},{128,112},... | collective-permute-start | bytes 589832 | tf_op jit(solution)/shard_map/ppermute | solution.py:25
  16.4 9.5 %copy-start.7 = (bf16[3,3,256,256]{3,2,1,0:T(8,128)(2,1)S(1)}, bf16[3,3,256,256]{3,2,1,0:T(8,128)(2,1)}, u32[]{:S(2)}) copy-start(bf16[3,3,256,256]{3,2,1,0:T(8,128)(2,1)} %param.10) | copy-start | bytes 3538948
  16.4 15.2 %collective-permute-start.2 = (bf16[2,4,48,256]{3,2,1,0:T(8,128)(2,1)}, bf16[2,4,48,256]{3,2,1,0:T(8,128)(2,1)S(1)}, u32[]{:S(2)}, u32[]{:S(2)}) collective-permute-start(bf16[2,4,48,256]{3,2,1,0:T(8,128)(2,1)} %slice_bitcast_fusion.1), channel_id=1, source_target_pairs={{0,16},{16,32},{32,48},{48,64},{64,80},{80,96},{96,112},{112,128},... | collective-permute-start | bytes 589832 | tf_op jit(solution)/shard_map/ppermute | solution.py:25
  20.3 16.8 %collective-permute-start = (bf16[4,1,48,512]{3,2,1,0:T(8,128)(2,1)}, bf16[4,1,48,512]{3,2,1,0:T(8,128)(2,1)}, u32[]{:S(2)}, u32[]{:S(2)}) collective-permute-start(bf16[4,1,48,512]{3,2,1,0:T(8,128)(2,1)} %get-tuple-element.37), channel_id=1, source_target_pairs={{0,2},{2,4},{4,6},{6,8},{8,10},{10,12},{12,14},{1,3},{3,5},{5,7},{... | collective-permute-start | bytes 589832 | tf_op jit(solution)/shard_map/ppermute | solution.py:16
  24.2 12.9 %collective-permute-start.1 = (bf16[4,1,48,512]{3,2,1,0:T(8,128)(2,1)}, bf16[4,1,48,512]{3,2,1,0:T(8,128)(2,1)}, u32[]{:S(2)}, u32[]{:S(2)}) collective-permute-start(bf16[4,1,48,512]{3,2,1,0:T(8,128)(2,1)} %get-tuple-element.38), channel_id=1, source_target_pairs={{2,0},{4,2},{6,4},{8,6},{10,8},{12,10},{14,12},{3,1},{5,3},{7,5},{... | collective-permute-start | bytes 589832 | tf_op jit(solution)/shard_map/ppermute | solution.py:17
  27.2 1.0 copy-start.27
  29.0 7.3 %copy-start.21 = (bf16[1,256,256]{1,2,0:T(8,128)(2,1)S(1)}, bf16[1,256,256]{1,2,0:T(8,128)(2,1)}, u32[]{:S(2)}) copy-start(bf16[1,256,256]{1,2,0:T(8,128)(2,1)} %copy.22) | copy-start | bytes 393220
  29.8 6.5 %copy-start.23 = (bf16[1,256,256]{1,2,0:T(8,128)(2,1)S(1)}, bf16[1,256,256]{1,2,0:T(8,128)(2,1)}, u32[]{:S(2)}) copy-start(bf16[1,256,256]{1,2,0:T(8,128)(2,1)} %copy.23) | copy-start | bytes 393220
  30.5 5.8 %copy-start.25 = (bf16[1,256,256]{1,2,0:T(8,128)(2,1)S(1)}, bf16[1,256,256]{1,2,0:T(8,128)(2,1)}, u32[]{:S(2)}) copy-start(bf16[1,256,256]{1,2,0:T(8,128)(2,1)} %copy.24) | copy-start | bytes 393220
  31.7 10.8 %collective-permute-start.4 = (bf16[2,1,48,512]{3,2,1,0:T(8,128)(2,1)S(1)}, bf16[2,1,48,512]{3,2,1,0:T(8,128)(2,1)S(1)}, u32[]{:S(2)}, u32[]{:S(2)}) collective-permute-start(bf16[2,1,48,512]{3,2,1,0:T(8,128)(2,1)S(1)} %get-tuple-element.48), channel_id=1, source_target_pairs={{0,2},{2,4},{4,6},{6,8},{8,10},{10,12},{12,14},{1,3},{3,5},{5,7},{... | collective-permute-start | bytes 294920 | tf_op jit(solution)/shard_map/ppermute | solution.py:16
  34.9 7.6 %collective-permute-start.5 = (bf16[2,1,48,512]{3,2,1,0:T(8,128)(2,1)S(1)}, bf16[2,1,48,512]{3,2,1,0:T(8,128)(2,1)S(1)}, u32[]{:S(2)}, u32[]{:S(2)}) collective-permute-start(bf16[2,1,48,512]{3,2,1,0:T(8,128)(2,1)S(1)} %get-tuple-element.49), channel_id=1, source_target_pairs={{2,0},{4,2},{6,4},{8,6},{10,8},{12,10},{14,12},{3,1},{5,3},{7,5},{... | collective-permute-start | bytes 294920 | tf_op jit(solution)/shard_map/ppermute | solution.py:17
  36.8 1.0 copy-start.5
  38.9 3.6 %copy-start.2 = (bf16[4,6,48,512]{3,2,1,0:T(8,128)(2,1)}, bf16[4,6,48,512]{3,2,1,0:T(8,128)(2,1)S(1)}, u32[]{:S(2)}) copy-start(bf16[4,6,48,512]{3,2,1,0:T(8,128)(2,1)S(1)} %pad_maximum_fusion) | copy-start | bytes 3538948
  40.1 1.3 copy-start.8
  42.5 0.7 copy-start.12
  42.5 1.2 slice-start
  45.6 0.9 slice-start.1
  45.6 1.1 copy-start.13
  46.8 0.8 copy-start.16
  46.8 0.9 copy-start.18
  255.8 4.3 %copy-start.4 = (bf16[3,256,256]{2,1,0:T(8,128)(2,1)S(1)}, bf16[3,256,256]{2,1,0:T(8,128)(2,1)}, u32[]{:S(2)}) copy-start(bf16[3,256,256]{2,1,0:T(8,128)(2,1)} %param.11) | copy-start | bytes 1179652
  255.8 4.3 %copy-start.15 = (bf16[1,2,48,256]{3,2,1,0:T(8,128)(2,1)S(1)}, bf16[1,2,48,256]{3,2,1,0:T(8,128)(2,1)}, u32[]{:S(2)}) copy-start(bf16[1,2,48,256]{3,2,1,0:T(8,128)(2,1)} %get-tuple-element.51) | copy-start | bytes 147460
  255.8 4.7 %copy-start.9 = (bf16[4,2,48,256]{3,2,1,0:T(8,128)(2,1)S(1)}, bf16[4,2,48,256]{3,2,1,0:T(8,128)(2,1)}, u32[]{:S(2)}) copy-start(bf16[4,2,48,256]{3,2,1,0:T(8,128)(2,1)} %get-tuple-element.52) | copy-start | bytes 589828
  255.8 4.7 %copy-start.10 = (bf16[4,2,48,256]{3,2,1,0:T(8,128)(2,1)S(1)}, bf16[4,2,48,256]{3,2,1,0:T(8,128)(2,1)}, u32[]{:S(2)}) copy-start(bf16[4,2,48,256]{3,2,1,0:T(8,128)(2,1)} %get-tuple-element.53) | copy-start | bytes 589828
  255.8 4.7 %copy-start.11 = (bf16[4,2,48,256]{3,2,1,0:T(8,128)(2,1)S(1)}, bf16[4,2,48,256]{3,2,1,0:T(8,128)(2,1)}, u32[]{:S(2)}) copy-start(bf16[4,2,48,256]{3,2,1,0:T(8,128)(2,1)} %get-tuple-element.54) | copy-start | bytes 589828
  257.7 2.9 %copy-start.22 = (bf16[1,256,256]{1,2,0:T(8,128)(2,1)S(1)}, bf16[1,256,256]{1,2,0:T(8,128)(2,1)}, u32[]{:S(2)}) copy-start(bf16[1,256,256]{1,2,0:T(8,128)(2,1)} %copy.22) | copy-start | bytes 393220
  257.7 2.9 %copy-start.24 = (bf16[1,256,256]{1,2,0:T(8,128)(2,1)S(1)}, bf16[1,256,256]{1,2,0:T(8,128)(2,1)}, u32[]{:S(2)}) copy-start(bf16[1,256,256]{1,2,0:T(8,128)(2,1)} %copy.23) | copy-start | bytes 393220
  257.7 2.9 %copy-start.26 = (bf16[1,256,256]{1,2,0:T(8,128)(2,1)S(1)}, bf16[1,256,256]{1,2,0:T(8,128)(2,1)}, u32[]{:S(2)}) copy-start(bf16[1,256,256]{1,2,0:T(8,128)(2,1)} %copy.24) | copy-start | bytes 393220
  260.1 0.8 copy-start.20
  261.8 1.0 copy-start.6
  261.9 1.1 copy-start.14
  261.9 1.2 copy-start.17
  261.9 1.3 copy-start.19
  263.2 1.2 copy-start.1
  263.2 1.4 copy-start.28

commit v5 on v4

--- a/solution.py
+++ b/solution.py
@@ -74,26 +74,12 @@
     inputs_prev = from_behind(inputs[frame_count - 2 :], "tm", 1)
     upstream_next = from_behind(upstream[:2], "tm", -1)
     local_both = extended(jnp.concatenate([inputs, upstream], axis=-1), (("height", 1),), 1)
-    rim_both = extended(
-        jnp.concatenate([inputs_prev, upstream_next], axis=-1), (("height", 1),), 1
-    )
 
     def spatial_forward(block):
         activ = jax.nn.silu(block.astype(jnp.float32)).astype(jnp.bfloat16)
         taps = forward_taps(jnp.pad(activ, ((0, 0), (0, 0), (1, 1), (0, 0))), row_count, col_count)
         out = flat_dot(taps, spatial_flat).astype(jnp.bfloat16)
         return taps, out.reshape(block.shape[0], row_count, col_count, channels)
-
-    activ_taps, spatial_out = spatial_forward(local_both[..., :channels])
-    unused, spatial_rim = spatial_forward(rim_both[..., :channels])
-    repeated = jnp.broadcast_to(spatial_out[:1], (2,) + spatial_out.shape[1:])
-    earlier = jnp.where(first_shard, repeated, spatial_rim)
-    padded_frames = jnp.concatenate([earlier, spatial_out], axis=0)
-    frame_stack = frame_taps(padded_frames, frame_count).reshape(-1, 3 * channels)
-    temporal_out = jnp.dot(frame_stack, temporal_flat, preferred_element_type=jnp.float32).reshape(
-        inputs.shape
-    )
-    decoded = (inputs.astype(jnp.float32) + temporal_out).astype(jnp.bfloat16)
 
     def frame_gradient(source):
         rows = source.shape[1]
@@ -107,7 +93,30 @@
         part = part.at[0].add(jnp.where(first_shard, fold, 0.0))
         return part.astype(jnp.bfloat16).reshape(frame_count, rows, col_count, channels)
 
+    activ_taps, spatial_out = spatial_forward(local_both[..., :channels])
     frame_grad = frame_gradient(jnp.concatenate([upstream, upstream_next], axis=0))
+    contract = (((0,), (0,)), ((), ()))
+    spatial_term = lax.dot_general(
+        activ_taps.reshape(-1, 9 * channels),
+        frame_grad.reshape(-1, channels),
+        contract,
+        preferred_element_type=jnp.float32,
+    )
+    rim_source = jnp.concatenate([inputs_prev, upstream_next], axis=-1)
+    spatial_out, spatial_term, rim_source = lax.optimization_barrier(
+        (spatial_out, spatial_term, rim_source)
+    )
+    rim_both = extended(rim_source, (("height", 1),), 1)
+    unused, spatial_rim = spatial_forward(rim_both[..., :channels])
+    repeated = jnp.broadcast_to(spatial_out[:1], (2,) + spatial_out.shape[1:])
+    earlier = jnp.where(first_shard, repeated, spatial_rim)
+    padded_frames = jnp.concatenate([earlier, spatial_out], axis=0)
+    frame_stack = frame_taps(padded_frames, frame_count).reshape(-1, 3 * channels)
+    temporal_out = jnp.dot(frame_stack, temporal_flat, preferred_element_type=jnp.float32).reshape(
+        inputs.shape
+    )
+    decoded = (inputs.astype(jnp.float32) + temporal_out).astype(jnp.bfloat16)
+
     up_rows = jnp.concatenate([local_both[..., channels:], rim_both[..., channels:]], axis=0)
     edge_grad = frame_gradient(jnp.stack([up_rows[:, 0], up_rows[:, row_count + 1]], axis=1))
     frame_grad_full = jnp.concatenate([edge_grad[:, :1], frame_grad, edge_grad[:, 1:]], axis=1)
@@ -126,11 +135,6 @@
         * lax.axis_size("dp")
     )
     grad_scale = 1.0 / math.sqrt(cell_count)
-    contract = (((0,), (0,)), ((), ()))
-    local_taps = activ_taps.reshape(-1, 9 * channels)
-    spatial_term = lax.dot_general(
-        local_taps, frame_grad.reshape(-1, channels), contract, preferred_element_type=jnp.float32
-    )
     temporal_term = lax.dot_general(
         frame_stack, upstream.reshape(-1, channels), contract, preferred_element_type=jnp.float32
     )

time: 268 us -> 280 us (1.045)
  local copies, waits for them, and re-layouts: 18.7 us -> 23.4 us
  blocking collectives: 207 us -> 211 us
  waiting for transfers between devices: 1.1 us -> 4.03 us
    unnamed x101 -> x94, local copies, waits for them, and re-layouts: 9.24 us -> 14.2 us
    psum x1, blocking collectives: 207 us -> 211 us  [local(): summed = lax.psum(weight_terms, ('tm', 'height', 'dp')).astype(jnp.bfloat16)]
    ppermute x2, waiting for transfers between devices: 0.01 us -> 3.73 us  [extended(): after = lax.ppermute(initial, axis, down)]
  transfers between devices with their start and end apart: 6 -> 6, of which waited for: 1 -> 2; matrix products, arithmetic and copies ran while one was open for 5% -> 7% of each run, Pallas kernels for 0% -> 0%
where the time goes in v5:
time: 280 us
  blocking collectives  211 us (75%)
  starting transfers between devices  25.6 us (9%)
  local copies, waits for them, and re-layouts  23.4 us (8%)
  matrix products  8.55 us (3%)
  other arithmetic  5.6 us (2%)
  waiting for transfers between devices  4.03 us (1%)
    psum x1, blocking collectives, local(): summed = lax.psum(weight_terms, ('tm', 'height', 'dp')).astype(jnp.bfloat16)  211 us
    ppermute x2, starting transfers between devices, from_behind(): return lax.ppermute(block, axis, route)  15.2 us
    unnamed x94, local copies, waits for them, and re-layouts  14.2 us
    ppermute x2, starting transfers between devices, extended(): before = lax.ppermute(last, axis, up)  7.87 us
  transfers between devices with their start and end apart: 6, of which 2 were waited for; matrix products, arithmetic and copies ran while one was open for 7% of the time, Pallas kernels for 0%

profile of v5, /device:TPU:7, one launch (start us, length us, event | category | flops | bytes accessed | tf_op | source)
XLA Modules:
  0.0 279.7 jit_solution(5824990904051708866)
XLA Ops:
  0.7 1.9 pad_maximum_fusion.8
  2.5 3.9 %collective-permute-start = (bf16[4,1,48,512]{3,2,1,0:T(8,128)(2,1)}, bf16[4,1,48,512]{3,2,1,0:T(8,128)(2,1)}, u32[]{:S(2)}, u32[]{:S(2)}) collective-permute-start(bf16[4,1,48,512]{3,2,1,0:T(8,128)(2,1)} %get-tuple-element.43), channel_id=1, source_target_pairs={{0,2},{2,4},{4,6},{6,8},{8,10},{10,12},{12,14},{1,3},{3,5},{5,7},{... | collective-permute-start | bytes 589832 | tf_op jit(solution)/shard_map/ppermute | solution.py:16
  6.4 1.3 collective-permute-start.1
  7.7 1.6 slice_bitcast_fusion.1
  9.3 13.3 %collective-permute-start.2 = (bf16[2,4,48,256]{3,2,1,0:T(8,128)(2,1)}, bf16[2,4,48,256]{3,2,1,0:T(8,128)(2,1)S(1)}, u32[]{:S(2)}, u32[]{:S(2)}) collective-permute-start(bf16[2,4,48,256]{3,2,1,0:T(8,128)(2,1)} %slice_bitcast_fusion.1), channel_id=1, source_target_pairs={{16,0},{32,16},{48,32},{64,48},{80,64},{96,80},{112,96},{128,112},... | collective-permute-start | bytes 589832 | tf_op jit(solution)/shard_map/ppermute | solution.py:25
  22.6 1.6 slice_bitcast_fusion
  24.2 1.9 collective-permute-start.3
  26.1 0.7 fusion.85
  26.8 0.8 copy.22
  27.6 0.8 copy.23
  28.4 0.8 copy.24
  29.1 0.2 fusion.70
  29.3 0.2 convolution_add_fusion.2
  29.8 0.7 bitcast_dynamic-update-slice_fusion.8
  31.3 0.7 bitcast_dynamic-update-slice_fusion.7
  31.9 0.6 bitcast_dynamic-update-slice_fusion.6
  32.6 0.7 bitcast_dynamic-update-slice_fusion.5
  33.2 0.6 bitcast_dynamic-update-slice_fusion.4
  33.9 0.7 bitcast_dynamic-update-slice_fusion.3
  34.5 0.7 bitcast_dynamic-update-slice_fusion.2
  35.2 0.6 bitcast_dynamic-update-slice_fusion.1
  35.8 0.7 bitcast_dynamic-update-slice_fusion
  36.5 1.1 pad_maximum_fusion.1
  37.7 0.4 fusion.9
  38.2 0.1 fusion.44
  38.3 0.1 fusion.45
  38.5 0.1 fusion.46
  38.6 0.1 fusion.47
  39.0 0.7 copy-done.18
  39.8 0.5 fusion.12
  40.2 0.4 copy-done.17
  40.6 0.2 fusion.63
  40.9 1.1 fusion.90
  42.1 0.1 copy-done.14
  42.2 1.1 convolution_convert_fusion
  43.3 1.1 pad_maximum_fusion.6
  44.4 4.0 %collective-permute-start.4 = (bf16[2,1,48,512]{3,2,1,0:T(8,128)(2,1)S(1)}, bf16[2,1,48,512]{3,2,1,0:T(8,128)(2,1)S(1)}, u32[]{:S(2)}, u32[]{:S(2)}) collective-permute-start(bf16[2,1,48,512]{3,2,1,0:T(8,128)(2,1)S(1)} %get-tuple-element.48), channel_id=1, source_target_pairs={{0,2},{2,4},{4,6},{6,8},{8,10},{10,12},{12,14},{1,3},{3,5},{5,7},{... | collective-permute-start | bytes 294920 | tf_op jit(solution)/shard_map/ppermute | solution.py:16
  48.5 1.3 collective-permute-start.5
  49.8 0.3 collective-permute-done.4
  50.1 3.7 %collective-permute-done.5 = bf16[2,1,48,512]{3,2,1,0:T(8,128)(2,1)S(1)} collective-permute-done((bf16[2,1,48,512]{3,2,1,0:T(8,128)(2,1)S(1)}, bf16[2,1,48,512]{3,2,1,0:T(8,128)(2,1)S(1)}, u32[]{:S(2)}, u32[]{:S(2)}) %collective-permute-start.5) | collective-permute-done | bytes 98336 | tf_op jit(solution)/shard_map/ppermute | solution.py:17
  53.8 0.2 fusion.38
  54.4 0.3 copy-done.15
  54.7 0.6 convolution_convert_fusion.1
  55.6 0.5 copy-done.9
  56.1 0.1 copy-done.11
  56.2 0.5 fusion.91
  56.7 0.3 maximum_multiply_fusion
  57.0 211.1 %all-reduce.4 = bf16[3072,256]{1,0:T(8,128)(2,1)} all-reduce(f32[3072,256]{1,0:T(8,128)S(1)} %maximum_multiply_fusion), channel_id=1, replica_groups=mesh['tm'=32,'height'=8,'dp'=2] {'tm','height','dp'}, use_global_device_ids=true, to_apply=%region_0.1 | all-reduce | flops 786432 | bytes 4718592 | tf_op jit(solution)/shard_map/psum | solution.py:142
  268.1 2.5 slice.367
  270.6 1.8 slice.368
  272.5 0.8 copy-done.4
  273.4 0.2 fusion.67
  273.5 0.2 convolution_add_fusion.4
  273.8 0.3 fusion.56
  274.2 0.2 fusion.24
  274.4 0.3 fusion.34
  274.9 0.1 slice_dynamic-update-slice_fusion.3
  275.2 0.1 slice_dynamic-update-slice_fusion.1
  275.4 0.7 copy-done.6
  276.1 0.1 copy-done.8
  276.2 0.1 copy-done.12
  276.4 1.2 fusion.4
  277.6 0.2 copy-done.24
  277.8 1.9 fusion.5
  (94 shorter events, 2.7 us)
Async XLA Ops:
  0.6 25.5 %copy-start = (bf16[1,4,4,48,256]{4,3,2,1,0:T(8,128)(2,1)S(1)}, bf16[1,4,4,48,256]{4,3,2,1,0:T(8,128)(2,1)}, u32[]{:S(2)}) copy-start(bf16[1,4,4,48,256]{4,3,2,1,0:T(8,128)(2,1)} %param.9) | copy-start | bytes 1179652
  0.6 26.2 %copy-start.3 = (bf16[3,256,256]{2,1,0:T(8,128)(2,1)S(1)}, bf16[3,256,256]{2,1,0:T(8,128)(2,1)}, u32[]{:S(2)}) copy-start(bf16[3,256,256]{2,1,0:T(8,128)(2,1)} %param.11) | copy-start | bytes 1179652
  2.5 34.0 %collective-permute-start = (bf16[4,1,48,512]{3,2,1,0:T(8,128)(2,1)}, bf16[4,1,48,512]{3,2,1,0:T(8,128)(2,1)}, u32[]{:S(2)}, u32[]{:S(2)}) collective-permute-start(bf16[4,1,48,512]{3,2,1,0:T(8,128)(2,1)} %get-tuple-element.43), channel_id=1, source_target_pairs={{0,2},{2,4},{4,6},{6,8},{8,10},{10,12},{12,14},{1,3},{3,5},{5,7},{... | collective-permute-start | bytes 589832 | tf_op jit(solution)/shard_map/ppermute | solution.py:16
  6.4 30.1 %collective-permute-start.1 = (bf16[4,1,48,512]{3,2,1,0:T(8,128)(2,1)}, bf16[4,1,48,512]{3,2,1,0:T(8,128)(2,1)}, u32[]{:S(2)}, u32[]{:S(2)}) collective-permute-start(bf16[4,1,48,512]{3,2,1,0:T(8,128)(2,1)} %get-tuple-element.44), channel_id=1, source_target_pairs={{2,0},{4,2},{6,4},{8,6},{10,8},{12,10},{14,12},{3,1},{5,3},{7,5},{... | collective-permute-start | bytes 589832 | tf_op jit(solution)/shard_map/ppermute | solution.py:17
  9.3 20.2 %copy-start.13 = (bf16[3,3,256,256]{3,2,1,0:T(8,128)(2,1)S(1)}, bf16[3,3,256,256]{3,2,1,0:T(8,128)(2,1)}, u32[]{:S(2)}) copy-start(bf16[3,3,256,256]{3,2,1,0:T(8,128)(2,1)} %param.10) | copy-start | bytes 3538948
  9.3 29.6 %collective-permute-start.2 = (bf16[2,4,48,256]{3,2,1,0:T(8,128)(2,1)}, bf16[2,4,48,256]{3,2,1,0:T(8,128)(2,1)S(1)}, u32[]{:S(2)}, u32[]{:S(2)}) collective-permute-start(bf16[2,4,48,256]{3,2,1,0:T(8,128)(2,1)} %slice_bitcast_fusion.1), channel_id=1, source_target_pairs={{16,0},{32,16},{48,32},{64,48},{80,64},{96,80},{112,96},{128,112},... | collective-permute-start | bytes 589832 | tf_op jit(solution)/shard_map/ppermute | solution.py:25
  24.2 19.1 %collective-permute-start.3 = (bf16[2,4,48,256]{3,2,1,0:T(8,128)(2,1)}, bf16[2,4,48,256]{3,2,1,0:T(8,128)(2,1)}, u32[]{:S(2)}, u32[]{:S(2)}) collective-permute-start(bf16[2,4,48,256]{3,2,1,0:T(8,128)(2,1)} %slice_bitcast_fusion), channel_id=1, source_target_pairs={{0,16},{16,32},{32,48},{48,64},{64,80},{80,96},{96,112},{112,128},... | collective-permute-start | bytes 589832 | tf_op jit(solution)/shard_map/ppermute | solution.py:25
  30.7 5.8 %copy-start.5 = (bf16[1,4,4,48,256]{4,3,2,1,0:T(8,128)(2,1)S(1)}, bf16[1,4,4,48,256]{4,3,2,1,0:T(8,128)(2,1)}, u32[]{:S(2)}) copy-start(bf16[1,4,4,48,256]{4,3,2,1,0:T(8,128)(2,1)} %param.8) | copy-start | bytes 1179652
  37.7 10.8 %copy-start.2 = (bf16[4,6,48,512]{3,2,1,0:T(8,128)(2,1)}, bf16[4,6,48,512]{3,2,1,0:T(8,128)(2,1)S(1)}, u32[]{:S(2)}) copy-start(bf16[4,6,48,512]{3,2,1,0:T(8,128)(2,1)S(1)} %pad_maximum_fusion.1) | copy-start | bytes 3538948
  38.7 0.9 copy-start.18
  38.7 1.0 copy-start.20
  38.7 1.0 copy-start.22
  39.7 0.9 copy-start.17
  40.9 1.3 copy-start.14
  43.3 12.2 %copy-start.7 = (bf16[768,256]{1,0:T(8,128)(2,1)}, bf16[768,256]{1,0:T(8,128)(2,1)S(1)}, u32[]{:S(2)}) copy-start(bf16[768,256]{1,0:T(8,128)(2,1)S(1)} %convolution_convert_fusion) | copy-start | bytes 1179652
  44.4 5.6 %collective-permute-start.4 = (bf16[2,1,48,512]{3,2,1,0:T(8,128)(2,1)S(1)}, bf16[2,1,48,512]{3,2,1,0:T(8,128)(2,1)S(1)}, u32[]{:S(2)}, u32[]{:S(2)}) collective-permute-start(bf16[2,1,48,512]{3,2,1,0:T(8,128)(2,1)S(1)} %get-tuple-element.48), channel_id=1, source_target_pairs={{0,2},{2,4},{4,6},{6,8},{8,10},{10,12},{12,14},{1,3},{3,5},{5,7},{... | collective-permute-start | bytes 294920 | tf_op jit(solution)/shard_map/ppermute | solution.py:16
  48.5 5.4 %collective-permute-start.5 = (bf16[2,1,48,512]{3,2,1,0:T(8,128)(2,1)S(1)}, bf16[2,1,48,512]{3,2,1,0:T(8,128)(2,1)S(1)}, u32[]{:S(2)}, u32[]{:S(2)}) collective-permute-start(bf16[2,1,48,512]{3,2,1,0:T(8,128)(2,1)S(1)} %get-tuple-element.47), channel_id=1, source_target_pairs={{2,0},{4,2},{6,4},{8,6},{10,8},{12,10},{14,12},{3,1},{5,3},{7,5},{... | collective-permute-start | bytes 294920 | tf_op jit(solution)/shard_map/ppermute | solution.py:17
  53.8 0.8 copy-start.15
  55.4 0.7 copy-start.9
  55.5 0.7 copy-start.11
  268.1 4.2 %copy-start.16 = (bf16[2,6,48,512]{3,2,1,0:T(8,128)(2,1)S(1)}, bf16[2,6,48,512]{3,2,1,0:T(8,128)(2,1)}, u32[]{:S(2)}) copy-start(bf16[2,6,48,512]{3,2,1,0:T(8,128)(2,1)} %copy-done.15) | copy-start | bytes 1769476
  268.1 4.3 %slice-start = ((bf16[4,6,48,512]{3,2,1,0:T(8,128)(2,1)}), bf16[4,6,48,256]{3,2,1,0:T(8,128)(2,1)S(1)}, s32[]{:S(2)}) async-start(bf16[4,6,48,512]{3,2,1,0:T(8,128)(2,1)} %copy-done.2), calls=%async_computation | async-start | bytes 1179648 | tf_op jit(solution)/shard_map/slice | solution.py:120
  272.4 1.0 copy-start.4
  272.4 1.4 copy-start.19
  272.4 1.4 copy-start.21
  272.4 1.4 copy-start.23
  275.1 1.0 copy-start.6
  275.1 1.1 copy-start.8
  275.1 1.1 copy-start.10
  275.1 1.3 copy-start.12
  276.4 1.2 copy-start.1
  276.4 1.4 copy-start.24

commit v6 on v4

--- a/solution.py
+++ b/solution.py
@@ -110,10 +110,17 @@
     frame_grad = frame_gradient(jnp.concatenate([upstream, upstream_next], axis=0))
     up_rows = jnp.concatenate([local_both[..., channels:], rim_both[..., channels:]], axis=0)
     edge_grad = frame_gradient(jnp.stack([up_rows[:, 0], up_rows[:, row_count + 1]], axis=1))
-    frame_grad_full = jnp.concatenate([edge_grad[:, :1], frame_grad, edge_grad[:, 1:]], axis=1)
-    grad_pad = jnp.pad(frame_grad_full, ((0, 0), (0, 0), (1, 1), (0, 0)))
+    grad_pad = jnp.pad(frame_grad, ((0, 0), (1, 1), (1, 1), (0, 0)))
     act_grad = flat_dot(backward_taps(grad_pad, row_count, col_count), spatial_back)
     act_grad = act_grad.reshape(inputs.shape)
+    edge_pad = jnp.pad(edge_grad, ((0, 0), (0, 0), (1, 1), (0, 0)))
+    edge_pad = jnp.concatenate(
+        [edge_pad[:, :1], jnp.zeros_like(edge_pad), edge_pad[:, 1:]], axis=1
+    )
+    edge_part = flat_dot(backward_taps(edge_pad, 2, col_count), spatial_back)
+    edge_part = edge_part.reshape(frame_count, 2, col_count, channels)
+    act_grad = act_grad.at[:, 0].add(edge_part[:, 0])
+    act_grad = act_grad.at[:, row_count - 1].add(edge_part[:, 1])
     input_grad = (
         upstream.astype(jnp.float32) + silu_slope(inputs.astype(jnp.float32)) * act_grad
     ).astype(jnp.bfloat16)

time: 268 us -> 275 us (1.026)
  local copies, waits for them, and re-layouts: 18.7 us -> 24.3 us
    unnamed x101 -> x122, local copies, waits for them, and re-layouts: 9.24 us -> 12.3 us
  transfers between devices with their start and end apart: 6 -> 6, of which waited for: 1 -> 0; matrix products, arithmetic and copies ran while one was open for 5% -> 7% of each run, Pallas kernels for 0% -> 0%
where the time goes in v6:
time: 275 us; the launch traced here: 272 us
  blocking collectives  206 us (75%)
  starting transfers between devices  25.6 us (9%)
  local copies, waits for them, and re-layouts  24.3 us (9%)
  matrix products  9.22 us (3%)
  other arithmetic  5.27 us (2%)
    psum x1, blocking collectives, local(): summed = lax.psum(weight_terms, ('tm', 'height', 'dp')).astype(jnp.bfloat16)  206 us
    ppermute x2, starting transfers between devices, from_behind(): return lax.ppermute(block, axis, route)  15.2 us
    unnamed x122, local copies, waits for them, and re-layouts  12.3 us
    ppermute x2, starting transfers between devices, extended(): before = lax.ppermute(last, axis, up)  7.87 us
  transfers between devices with their start and end apart: 6, of which 0 were waited for; matrix products, arithmetic and copies ran while one was open for 7% of the time, Pallas kernels for 0%

profile of v6, /device:TPU:7, one launch (start us, length us, event | category | flops | bytes accessed | tf_op | source)
XLA Modules:
  0.0 272.5 jit_solution(6811536912322276533)
XLA Ops:
  0.7 1.7 slice_bitcast_fusion
  2.3 13.1 %collective-permute-start.3 = (bf16[2,4,48,256]{3,2,1,0:T(8,128)(2,1)}, bf16[2,4,48,256]{3,2,1,0:T(8,128)(2,1)S(1)}, u32[]{:S(2)}, u32[]{:S(2)}) collective-permute-start(bf16[2,4,48,256]{3,2,1,0:T(8,128)(2,1)} %slice_bitcast_fusion), channel_id=1, source_target_pairs={{16,0},{32,16},{48,32},{64,48},{80,64},{96,80},{112,96},{128,112},... | collective-permute-start | bytes 589832 | tf_op jit(solution)/shard_map/ppermute | solution.py:25
  15.5 1.6 slice_bitcast_fusion.1
  17.1 2.0 collective-permute-start.2
  19.2 1.8 pad_maximum_fusion.6
  21.0 3.9 %collective-permute-start = (bf16[4,1,48,512]{3,2,1,0:T(8,128)(2,1)}, bf16[4,1,48,512]{3,2,1,0:T(8,128)(2,1)}, u32[]{:S(2)}, u32[]{:S(2)}) collective-permute-start(bf16[4,1,48,512]{3,2,1,0:T(8,128)(2,1)} %get-tuple-element.61), channel_id=1, source_target_pairs={{0,2},{2,4},{4,6},{6,8},{8,10},{10,12},{12,14},{1,3},{3,5},{5,7},{... | collective-permute-start | bytes 589832 | tf_op jit(solution)/shard_map/ppermute | solution.py:16
  24.9 1.3 collective-permute-start.1
  26.2 0.7 fusion.106
  26.8 0.8 fusion.107
  27.6 0.2 fusion.91
  27.8 0.2 convolution_add_fusion.2
  28.1 0.8 copy.33
  29.0 0.1 copy.31
  29.2 0.8 copy.29
  30.0 0.8 copy.28
  31.1 1.0 bitcast_dynamic-update-slice_fusion.5
  32.3 1.0 copy-done.32
  33.7 1.0 constant_dynamic-update-slice_fusion.1
  34.7 4.0 %collective-permute-start.4 = (bf16[2,1,48,512]{3,2,1,0:T(8,128)(2,1)S(1)}, bf16[2,1,48,512]{3,2,1,0:T(8,128)(2,1)S(1)}, u32[]{:S(2)}, u32[]{:S(2)}) collective-permute-start(bf16[2,1,48,512]{3,2,1,0:T(8,128)(2,1)S(1)} %get-tuple-element.72), channel_id=1, source_target_pairs={{0,2},{2,4},{4,6},{6,8},{8,10},{10,12},{12,14},{1,3},{3,5},{5,7},{... | collective-permute-start | bytes 294920 | tf_op jit(solution)/shard_map/ppermute | solution.py:16
  38.7 1.3 collective-permute-start.5
  40.1 0.5 fusion.11
  40.6 0.4 copy-done.24
  41.0 0.2 fusion.84
  41.3 0.3 copy-done.1
  41.6 1.1 pad_maximum_fusion
  42.8 0.4 fusion.5
  43.2 0.1 fusion.49
  43.3 0.1 fusion.50
  43.4 0.1 fusion.51
  43.6 0.1 fusion.52
  43.7 0.1 fusion.53
  43.9 0.1 fusion.54
  44.0 1.1 convolution_convert_fusion
  45.1 1.1 fusion.111
  46.4 0.1 fusion.60
  46.6 0.1 fusion.61
  46.9 0.9 copy-done.33
  47.9 2.0 fusion.25
  49.9 0.2 fusion.44
  50.1 0.8 slice-done
  50.9 0.7 fusion.109
  51.6 0.9 fusion.110
  52.9 0.6 convolution_convert_fusion.1
  53.5 0.2 slice-done.1
  53.8 0.2 copy-done.12
  54.0 0.8 copy-done.20
  54.7 0.1 copy-done.22
  54.8 0.5 fusion.17
  55.4 0.3 maximum_multiply_fusion
  55.6 206.5 %all-reduce.7 = bf16[3072,256]{1,0:T(8,128)(2,1)} all-reduce(f32[3072,256]{1,0:T(8,128)S(1)} %maximum_multiply_fusion), channel_id=1, replica_groups=mesh['tm'=32,'height'=8,'dp'=2] {'tm','height','dp'}, use_global_device_ids=true, to_apply=%region_0.1 | all-reduce | flops 786432 | bytes 4718592 | tf_op jit(solution)/shard_map/psum | solution.py:145
  262.1 1.9 slice.461
  264.0 2.4 slice.460
  266.4 0.2 fusion.88
  266.5 0.2 convolution_add_fusion.4
  266.9 0.3 fusion.69
  267.2 0.2 fusion.32
  267.8 0.9 copy-done.34
  268.7 0.6 fusion.23
  269.4 0.3 copy-done.2
  269.7 0.1 copy-done.13
  269.8 0.1 copy-done.21
  269.9 0.1 copy-done.23
  270.1 1.2 fusion.1
  271.4 1.1 fusion.65
  (124 shorter events, 2.6 us)
Async XLA Ops:
  0.6 25.5 %copy-start = (bf16[1,4,4,48,256]{4,3,2,1,0:T(8,128)(2,1)S(1)}, bf16[1,4,4,48,256]{4,3,2,1,0:T(8,128)(2,1)}, u32[]{:S(2)}) copy-start(bf16[1,4,4,48,256]{4,3,2,1,0:T(8,128)(2,1)} %param.13) | copy-start | bytes 1179652
  0.6 26.2 %copy-start.4 = (bf16[3,256,256]{2,1,0:T(8,128)(2,1)S(1)}, bf16[3,256,256]{2,1,0:T(8,128)(2,1)}, u32[]{:S(2)}) copy-start(bf16[3,256,256]{2,1,0:T(8,128)(2,1)} %param.15) | copy-start | bytes 1179652
  2.3 32.3 %collective-permute-start.3 = (bf16[2,4,48,256]{3,2,1,0:T(8,128)(2,1)}, bf16[2,4,48,256]{3,2,1,0:T(8,128)(2,1)S(1)}, u32[]{:S(2)}, u32[]{:S(2)}) collective-permute-start(bf16[2,4,48,256]{3,2,1,0:T(8,128)(2,1)} %slice_bitcast_fusion), channel_id=1, source_target_pairs={{16,0},{32,16},{48,32},{64,48},{80,64},{96,80},{112,96},{128,112},... | collective-permute-start | bytes 589832 | tf_op jit(solution)/shard_map/ppermute | solution.py:25
  17.1 10.9 %copy-start.7 = (bf16[3,3,256,256]{3,2,1,0:T(8,128)(2,1)S(1)}, bf16[3,3,256,256]{3,2,1,0:T(8,128)(2,1)}, u32[]{:S(2)}) copy-start(bf16[3,3,256,256]{3,2,1,0:T(8,128)(2,1)} %param.14) | copy-start | bytes 3538948
  17.1 16.6 %collective-permute-start.2 = (bf16[2,4,48,256]{3,2,1,0:T(8,128)(2,1)}, bf16[2,4,48,256]{3,2,1,0:T(8,128)(2,1)}, u32[]{:S(2)}, u32[]{:S(2)}) collective-permute-start(bf16[2,4,48,256]{3,2,1,0:T(8,128)(2,1)} %slice_bitcast_fusion.1), channel_id=1, source_target_pairs={{0,16},{16,32},{32,48},{48,64},{64,80},{80,96},{96,112},{112,128},... | collective-permute-start | bytes 589832 | tf_op jit(solution)/shard_map/ppermute | solution.py:25
  21.0 20.3 %collective-permute-start = (bf16[4,1,48,512]{3,2,1,0:T(8,128)(2,1)}, bf16[4,1,48,512]{3,2,1,0:T(8,128)(2,1)}, u32[]{:S(2)}, u32[]{:S(2)}) collective-permute-start(bf16[4,1,48,512]{3,2,1,0:T(8,128)(2,1)} %get-tuple-element.61), channel_id=1, source_target_pairs={{0,2},{2,4},{4,6},{6,8},{8,10},{10,12},{12,14},{1,3},{3,5},{5,7},{... | collective-permute-start | bytes 589832 | tf_op jit(solution)/shard_map/ppermute | solution.py:16
  24.9 16.4 %collective-permute-start.1 = (bf16[4,1,48,512]{3,2,1,0:T(8,128)(2,1)}, bf16[4,1,48,512]{3,2,1,0:T(8,128)(2,1)}, u32[]{:S(2)}, u32[]{:S(2)}) collective-permute-start(bf16[4,1,48,512]{3,2,1,0:T(8,128)(2,1)} %get-tuple-element.62), channel_id=1, source_target_pairs={{2,0},{4,2},{6,4},{8,6},{10,8},{12,10},{14,12},{3,1},{5,3},{7,5},{... | collective-permute-start | bytes 589832 | tf_op jit(solution)/shard_map/ppermute | solution.py:17
  29.2 3.1 %copy-start.14 = (bf16[1,1,256,256]{2,3,1,0:T(8,128)(2,1)S(1)}, bf16[1,1,256,256]{2,3,1,0:T(8,128)(2,1)}, u32[]{:S(2)}) copy-start(bf16[1,1,256,256]{2,3,1,0:T(8,128)(2,1)} %copy.33) | copy-start | bytes 393220
  30.0 2.2 copy-start.15
  31.1 2.5 copy-start.16
  31.1 2.3 copy-start.17
  31.1 2.2 copy-start.18
  32.3 1.0 copy-start.32
  33.4 7.2 %copy-start.26 = (bf16[1,256,256]{1,2,0:T(8,128)(2,1)}, bf16[1,256,256]{1,2,0:T(8,128)(2,1)S(1)}, u32[]{:S(2)}) copy-start(bf16[1,256,256]{1,2,0:T(8,128)(2,1)S(1)} %copy.22) | copy-start | bytes 393220
  33.5 7.1 %copy-start.28 = (bf16[1,256,256]{1,2,0:T(8,128)(2,1)}, bf16[1,256,256]{1,2,0:T(8,128)(2,1)S(1)}, u32[]{:S(2)}) copy-start(bf16[1,256,256]{1,2,0:T(8,128)(2,1)S(1)} %copy.23) | copy-start | bytes 393220
  33.7 6.9 %copy-start.30 = (bf16[1,256,256]{1,2,0:T(8,128)(2,1)}, bf16[1,256,256]{1,2,0:T(8,128)(2,1)S(1)}, u32[]{:S(2)}) copy-start(bf16[1,256,256]{1,2,0:T(8,128)(2,1)S(1)} %copy.24) | copy-start | bytes 393220
  34.7 15.1 %collective-permute-start.4 = (bf16[2,1,48,512]{3,2,1,0:T(8,128)(2,1)S(1)}, bf16[2,1,48,512]{3,2,1,0:T(8,128)(2,1)S(1)}, u32[]{:S(2)}, u32[]{:S(2)}) collective-permute-start(bf16[2,1,48,512]{3,2,1,0:T(8,128)(2,1)S(1)} %get-tuple-element.72), channel_id=1, source_target_pairs={{0,2},{2,4},{4,6},{6,8},{8,10},{10,12},{12,14},{1,3},{3,5},{5,7},{... | collective-permute-start | bytes 294920 | tf_op jit(solution)/shard_map/ppermute | solution.py:16
  38.7 11.1 %collective-permute-start.5 = (bf16[2,1,48,512]{3,2,1,0:T(8,128)(2,1)S(1)}, bf16[2,1,48,512]{3,2,1,0:T(8,128)(2,1)S(1)}, u32[]{:S(2)}, u32[]{:S(2)}) collective-permute-start(bf16[2,1,48,512]{3,2,1,0:T(8,128)(2,1)S(1)} %get-tuple-element.73), channel_id=1, source_target_pairs={{2,0},{4,2},{6,4},{8,6},{10,8},{12,10},{14,12},{3,1},{5,3},{7,5},{... | collective-permute-start | bytes 294920 | tf_op jit(solution)/shard_map/ppermute | solution.py:17
  40.1 0.9 copy-start.24
  40.6 1.0 copy-start.1
  42.8 7.0 %copy-start.3 = (bf16[4,6,48,512]{3,2,1,0:T(8,128)(2,1)}, bf16[4,6,48,512]{3,2,1,0:T(8,128)(2,1)S(1)}, u32[]{:S(2)}) copy-start(bf16[4,6,48,512]{3,2,1,0:T(8,128)(2,1)S(1)} %pad_maximum_fusion) | copy-start | bytes 3538948
  45.1 4.8 %copy-start.11 = (bf16[768,256]{1,0:T(8,128)(2,1)}, bf16[768,256]{1,0:T(8,128)(2,1)S(1)}, u32[]{:S(2)}) copy-start(bf16[768,256]{1,0:T(8,128)(2,1)S(1)} %convolution_convert_fusion) | copy-start | bytes 1179652
  46.6 1.3 copy-start.33
  49.8 1.1 slice-start
  52.8 0.9 slice-start.1
  52.8 1.1 copy-start.12
  54.0 0.8 copy-start.20
  54.0 0.9 copy-start.22
  262.1 4.3 %copy-start.5 = (bf16[3,256,256]{2,1,0:T(8,128)(2,1)S(1)}, bf16[3,256,256]{2,1,0:T(8,128)(2,1)}, u32[]{:S(2)}) copy-start(bf16[3,256,256]{2,1,0:T(8,128)(2,1)} %param.15) | copy-start | bytes 1179652
  262.1 4.3 %copy-start.19 = (bf16[1,2,48,256]{3,2,1,0:T(8,128)(2,1)S(1)}, bf16[1,2,48,256]{3,2,1,0:T(8,128)(2,1)}, u32[]{:S(2)}) copy-start(bf16[1,2,48,256]{3,2,1,0:T(8,128)(2,1)} %get-tuple-element.75) | copy-start | bytes 147460
  262.1 4.7 %copy-start.8 = (bf16[4,2,48,256]{3,2,1,0:T(8,128)(2,1)S(1)}, bf16[4,2,48,256]{3,2,1,0:T(8,128)(2,1)}, u32[]{:S(2)}) copy-start(bf16[4,2,48,256]{3,2,1,0:T(8,128)(2,1)} %get-tuple-element.76) | copy-start | bytes 589828
  262.1 4.7 %copy-start.9 = (bf16[4,2,48,256]{3,2,1,0:T(8,128)(2,1)S(1)}, bf16[4,2,48,256]{3,2,1,0:T(8,128)(2,1)}, u32[]{:S(2)}) copy-start(bf16[4,2,48,256]{3,2,1,0:T(8,128)(2,1)} %get-tuple-element.77) | copy-start | bytes 589828
  262.1 4.7 %copy-start.10 = (bf16[4,2,48,256]{3,2,1,0:T(8,128)(2,1)S(1)}, bf16[4,2,48,256]{3,2,1,0:T(8,128)(2,1)}, u32[]{:S(2)}) copy-start(bf16[4,2,48,256]{3,2,1,0:T(8,128)(2,1)} %get-tuple-element.78) | copy-start | bytes 589828
  264.0 2.9 %copy-start.27 = (bf16[1,256,256]{1,2,0:T(8,128)(2,1)S(1)}, bf16[1,256,256]{1,2,0:T(8,128)(2,1)}, u32[]{:S(2)}) copy-start(bf16[1,256,256]{1,2,0:T(8,128)(2,1)} %copy-done.26) | copy-start | bytes 393220
  264.0 2.9 %copy-start.29 = (bf16[1,256,256]{1,2,0:T(8,128)(2,1)S(1)}, bf16[1,256,256]{1,2,0:T(8,128)(2,1)}, u32[]{:S(2)}) copy-start(bf16[1,256,256]{1,2,0:T(8,128)(2,1)} %copy-done.28) | copy-start | bytes 393220
  264.0 2.9 %copy-start.31 = (bf16[1,256,256]{1,2,0:T(8,128)(2,1)S(1)}, bf16[1,256,256]{1,2,0:T(8,128)(2,1)}, u32[]{:S(2)}) copy-start(bf16[1,256,256]{1,2,0:T(8,128)(2,1)} %copy-done.30) | copy-start | bytes 393220
  266.4 0.8 copy-start.25
  267.4 1.3 copy-start.34
  268.7 1.0 copy-start.2
  268.7 1.1 copy-start.13
  268.7 1.2 copy-start.21
  268.7 1.3 copy-start.23
  270.1 1.2 copy-start.6

commit v7 on v4

--- a/solution.py
+++ b/solution.py
@@ -23,6 +23,17 @@
     devices = range(lax.axis_size(axis))
     route = [(i - distance, i) for i in devices if i - distance in devices]
     return lax.ppermute(block, axis, route)
+
+
+def diagonal(block, frame_step, row_step):
+    frames, rows = (lax.axis_size("tm"), lax.axis_size("height"))
+    route = [
+        (t * rows + h, (t + frame_step) * rows + h + row_step)
+        for t in range(frames)
+        for h in range(rows)
+        if 0 <= t + frame_step < frames and 0 <= h + row_step < rows
+    ]
+    return lax.ppermute(block, ("tm", "height"), route)
 
 
 def silu_slope(values):
@@ -74,8 +85,21 @@
     inputs_prev = from_behind(inputs[frame_count - 2 :], "tm", 1)
     upstream_next = from_behind(upstream[:2], "tm", -1)
     local_both = extended(jnp.concatenate([inputs, upstream], axis=-1), (("height", 1),), 1)
-    rim_both = extended(
-        jnp.concatenate([inputs_prev, upstream_next], axis=-1), (("height", 1),), 1
+    rim_in = jnp.concatenate(
+        [
+            diagonal(inputs[frame_count - 2 :, row_count - 1 :], 1, 1),
+            inputs_prev,
+            diagonal(inputs[frame_count - 2 :, :1], 1, -1),
+        ],
+        axis=1,
+    )
+    rim_up = jnp.concatenate(
+        [
+            diagonal(upstream[:2, row_count - 1 :], -1, 1),
+            upstream_next,
+            diagonal(upstream[:2, :1], -1, -1),
+        ],
+        axis=1,
     )
 
     def spatial_forward(block):
@@ -85,7 +109,7 @@
         return taps, out.reshape(block.shape[0], row_count, col_count, channels)
 
     activ_taps, spatial_out = spatial_forward(local_both[..., :channels])
-    unused, spatial_rim = spatial_forward(rim_both[..., :channels])
+    unused, spatial_rim = spatial_forward(rim_in)
     repeated = jnp.broadcast_to(spatial_out[:1], (2,) + spatial_out.shape[1:])
     earlier = jnp.where(first_shard, repeated, spatial_rim)
     padded_frames = jnp.concatenate([earlier, spatial_out], axis=0)
@@ -108,7 +132,7 @@
         return part.astype(jnp.bfloat16).reshape(frame_count, rows, col_count, channels)
 
     frame_grad = frame_gradient(jnp.concatenate([upstream, upstream_next], axis=0))
-    up_rows = jnp.concatenate([local_both[..., channels:], rim_both[..., channels:]], axis=0)
+    up_rows = jnp.concatenate([local_both[..., channels:], rim_up], axis=0)
     edge_grad = frame_gradient(jnp.stack([up_rows[:, 0], up_rows[:, row_count + 1]], axis=1))
     frame_grad_full = jnp.concatenate([edge_grad[:, :1], frame_grad, edge_grad[:, 1:]], axis=1)
     grad_pad = jnp.pad(frame_grad_full, ((0, 0), (0, 0), (1, 1), (0, 0)))

time: 268 us -> 287 us (1.071)
  waiting for transfers between devices: 1.1 us -> 16.3 us
  blocking collectives: 207 us -> 192 us
  local copies, waits for them, and re-layouts: 18.7 us -> 30.9 us
  starting transfers between devices: 24.8 us -> 30.4 us
    ppermute x0 -> x4, starting transfers between devices: none -> 20.1 us  [diagonal(): return lax.ppermute(block, ('tm', 'height'), route)]
    psum x1, blocking collectives: 207 us -> 192 us  [local(): summed = lax.psum(weight_terms, ('tm', 'height', 'dp')).astype(jnp.bfloat16)]
    ppermute x2, waiting for transfers between devices: 1.09 us -> 16.3 us  [from_behind(): return lax.ppermute(block, axis, route)]
    ppermute x2, starting transfers between devices: 15.2 us -> 5.74 us  [from_behind(): return lax.ppermute(block, axis, route)]
    unnamed x101 -> x100, local copies, waits for them, and re-layouts: 9.24 us -> 18.2 us
    ppermute x2 -> x1, starting transfers between devices: 7.08 us -> 3.29 us  [extended(): before = lax.ppermute(last, axis, up)]
  transfers between devices with their start and end apart: 6 -> 8, of which waited for: 1 -> 1; matrix products, arithmetic and copies ran while one was open for 5% -> 9% of each run, Pallas kernels for 0% -> 0%
where the time goes in v7:
time: 287 us; the launch traced here: 284 us
  blocking collectives  192 us (67%)
  local copies, waits for them, and re-layouts  30.9 us (11%)
  starting transfers between devices  30.4 us (11%)
  waiting for transfers between devices  16.3 us (6%)
  matrix products  8.57 us (3%)
  other arithmetic  5.19 us (2%)
    psum x1, blocking collectives, local(): summed = lax.psum(weight_terms, ('tm', 'height', 'dp')).astype(jnp.bfloat16)  192 us
    ppermute x4, starting transfers between devices, diagonal(): return lax.ppermute(block, ('tm', 'height'), route)  20.1 us
    unnamed x100, local copies, waits for them, and re-layouts  18.2 us
    ppermute x2, waiting for transfers between devices, from_behind(): return lax.ppermute(block, axis, route)  16.3 us
    ppermute x2, starting transfers between devices, from_behind(): return lax.ppermute(block, axis, route)  5.74 us
  transfers between devices with their start and end apart: 8, of which 1 were waited for; matrix products, arithmetic and copies ran while one was open for 9% of the time, Pallas kernels for 0%

profile of v7, /device:TPU:7, one launch (start us, length us, event | category | flops | bytes accessed | tf_op | source)
XLA Modules:
  0.0 284.5 jit_solution(11341409628747089263)
XLA Ops:
  0.7 1.5 fusion.103
  2.2 5.2 %collective-permute-start.2 = (bf16[2,1,48,256]{3,2,1,0:T(8,128)(2,1)}, bf16[2,1,48,256]{3,2,1,0:T(8,128)(2,1)}, u32[]{:S(2)}, u32[]{:S(2)}) collective-permute-start(bf16[2,1,48,256]{3,2,1,0:T(8,128)(2,1)} %get-tuple-element.50), channel_id=1, source_target_pairs={{0,18},{2,20},{4,22},{6,24},{8,26},{10,28},{12,30},{16,34},{18,36}... | collective-permute-start | bytes 147464 | tf_op jit(solution)/shard_map/ppermute | solution.py:36
  7.4 1.3 collective-permute-start.4
  8.6 1.5 fusion.102
  10.1 12.4 %collective-permute-start.5 = (bf16[2,1,48,256]{3,2,1,0:T(8,128)(2,1)}, bf16[2,1,48,256]{3,2,1,0:T(8,128)(2,1)S(1)}, u32[]{:S(2)}, u32[]{:S(2)}) collective-permute-start(bf16[2,1,48,256]{3,2,1,0:T(8,128)(2,1)} %get-tuple-element.48), channel_id=1, source_target_pairs={{16,2},{18,4},{20,6},{22,8},{24,10},{26,12},{28,14},{32,18},{34,20... | collective-permute-start | bytes 147464 | tf_op jit(solution)/shard_map/ppermute | solution.py:36
  22.5 1.8 pad_maximum_fusion.7
  24.3 3.3 %collective-permute-start = (bf16[4,1,48,512]{3,2,1,0:T(8,128)(2,1)}, bf16[4,1,48,512]{3,2,1,0:T(8,128)(2,1)}, u32[]{:S(2)}, u32[]{:S(2)}) collective-permute-start(bf16[4,1,48,512]{3,2,1,0:T(8,128)(2,1)} %get-tuple-element.37), channel_id=1, source_target_pairs={{0,2},{2,4},{4,6},{6,8},{8,10},{10,12},{12,14},{1,3},{3,5},{5,7},{... | collective-permute-start | bytes 589832 | tf_op jit(solution)/shard_map/ppermute | solution.py:16
  27.6 1.3 collective-permute-start.1
  28.9 1.6 slice_bitcast_fusion.1
  30.5 0.7 slice_bitcast_fusion
  31.2 0.6 fusion.100
  31.9 0.2 fusion.82
  32.1 0.2 convolution_add_fusion.2
  32.3 0.8 copy.22
  33.1 0.8 copy.23
  33.9 0.8 copy.24
  35.0 0.7 copy.30
  35.8 0.7 copy.29
  36.5 0.8 copy.28
  37.3 0.7 copy.27
  38.2 0.7 bitcast_dynamic-update-slice_fusion.8
  38.9 0.7 bitcast_dynamic-update-slice_fusion.7
  39.5 1.6 bitcast_dynamic-update-slice_fusion.6
  41.1 1.6 bitcast_dynamic-update-slice_fusion.5
  42.7 1.5 bitcast_dynamic-update-slice_fusion.4
  44.2 0.7 bitcast_dynamic-update-slice_fusion.3
  44.9 0.7 bitcast_dynamic-update-slice_fusion.2
  45.5 0.7 bitcast_dynamic-update-slice_fusion.1
  46.2 0.7 bitcast_dynamic-update-slice_fusion
  46.8 1.3 collective-permute-start.7
  48.2 3.8 %collective-permute-start.6 = (bf16[2,4,48,256]{3,2,1,0:T(8,128)(2,1)S(1)}, bf16[2,4,48,256]{3,2,1,0:T(8,128)(2,1)S(1)}, u32[]{:S(2)}, u32[]{:S(2)}) collective-permute-start(bf16[2,4,48,256]{3,2,1,0:T(8,128)(2,1)S(1)} %copy-done.20), channel_id=1, source_target_pairs={{16,0},{32,16},{48,32},{64,48},{80,64},{96,80},{112,96},{128,112},... | collective-permute-start | bytes 589832 | tf_op jit(solution)/shard_map/ppermute | solution.py:25
  52.0 1.1 pad_maximum_fusion
  53.2 0.4 fusion.9
  53.6 0.5 copy-done.19
  54.1 1.9 collective-permute-start.3
  56.1 0.9 fusion.105
  57.0 0.5 fusion.15
  57.5 0.4 copy-done.18
  57.9 0.2 fusion.78
  58.1 0.6 fusion.104
  58.8 16.3 %collective-permute-done.3 = bf16[2,4,48,256]{3,2,1,0:T(8,128)(2,1)S(1)} collective-permute-done((bf16[2,4,48,256]{3,2,1,0:T(8,128)(2,1)S(1)}, bf16[2,4,48,256]{3,2,1,0:T(8,128)(2,1)S(1)}, u32[]{:S(2)}, u32[]{:S(2)}) %collective-permute-start.3) | collective-permute-done | bytes 196640 | tf_op jit(solution)/shard_map/ppermute | solution.py:25
  75.1 1.0 fusion.47
  76.8 0.1 fusion.56
  77.0 0.1 fusion.58
  77.3 0.6 convolution_convert_fusion.1
  78.0 1.1 convolution_convert_fusion
  79.1 1.1 fusion.107
  80.4 0.7 copy-done.14
  81.2 0.5 fusion.21
  81.7 0.3 maximum_multiply_fusion
  82.0 191.8 %all-reduce.4 = bf16[3072,256]{1,0:T(8,128)(2,1)} all-reduce(f32[3072,256]{1,0:T(8,128)S(1)} %maximum_multiply_fusion), channel_id=1, replica_groups=mesh['tm'=32,'height'=8,'dp'=2] {'tm','height','dp'}, use_global_device_ids=true, to_apply=%region_0.1 | all-reduce | flops 786432 | bytes 4718592 | tf_op jit(solution)/shard_map/psum | solution.py:162
  273.8 1.9 slice.372
  275.6 2.4 slice.371
  278.0 0.2 fusion.85
  278.2 0.2 convolution_add_fusion.4
  278.5 0.3 fusion.71
  278.9 0.2 fusion.33
  279.1 0.3 fusion.43
  279.6 0.1 slice_dynamic-update-slice_fusion.3
  279.9 0.1 slice_dynamic-update-slice_fusion.1
  280.1 0.7 copy-done.5
  281.2 1.2 fusion.4
  282.4 0.2 copy-done.28
  282.6 1.9 fusion.5
  (100 shorter events, 2.7 us)
Async XLA Ops:
  0.6 29.9 %copy-start = (bf16[1,4,4,48,256]{4,3,2,1,0:T(8,128)(2,1)S(1)}, bf16[1,4,4,48,256]{4,3,2,1,0:T(8,128)(2,1)}, u32[]{:S(2)}) copy-start(bf16[1,4,4,48,256]{4,3,2,1,0:T(8,128)(2,1)} %param.9) | copy-start | bytes 1179652
  0.6 31.2 %copy-start.2 = (bf16[3,256,256]{2,1,0:T(8,128)(2,1)S(1)}, bf16[3,256,256]{2,1,0:T(8,128)(2,1)}, u32[]{:S(2)}) copy-start(bf16[3,256,256]{2,1,0:T(8,128)(2,1)} %param.11) | copy-start | bytes 1179652
  2.2 56.6 %collective-permute-start.2 = (bf16[2,1,48,256]{3,2,1,0:T(8,128)(2,1)}, bf16[2,1,48,256]{3,2,1,0:T(8,128)(2,1)}, u32[]{:S(2)}, u32[]{:S(2)}) collective-permute-start(bf16[2,1,48,256]{3,2,1,0:T(8,128)(2,1)} %get-tuple-element.50), channel_id=1, source_target_pairs={{0,18},{2,20},{4,22},{6,24},{8,26},{10,28},{12,30},{16,34},{18,36}... | collective-permute-start | bytes 147464 | tf_op jit(solution)/shard_map/ppermute | solution.py:36
  7.4 51.5 %collective-permute-start.4 = (bf16[2,1,48,256]{3,2,1,0:T(8,128)(2,1)}, bf16[2,1,48,256]{3,2,1,0:T(8,128)(2,1)}, u32[]{:S(2)}, u32[]{:S(2)}) collective-permute-start(bf16[2,1,48,256]{3,2,1,0:T(8,128)(2,1)} %get-tuple-element.51), channel_id=1, source_target_pairs={{2,16},{4,18},{6,20},{8,22},{10,24},{12,26},{14,28},{18,32},{20,34... | collective-permute-start | bytes 147464 | tf_op jit(solution)/shard_map/ppermute | solution.py:36
  10.1 43.5 %collective-permute-start.5 = (bf16[2,1,48,256]{3,2,1,0:T(8,128)(2,1)}, bf16[2,1,48,256]{3,2,1,0:T(8,128)(2,1)S(1)}, u32[]{:S(2)}, u32[]{:S(2)}) collective-permute-start(bf16[2,1,48,256]{3,2,1,0:T(8,128)(2,1)} %get-tuple-element.48), channel_id=1, source_target_pairs={{16,2},{18,4},{20,6},{22,8},{24,10},{26,12},{28,14},{32,18},{34,20... | collective-permute-start | bytes 147464 | tf_op jit(solution)/shard_map/ppermute | solution.py:36
  24.3 22.5 %collective-permute-start = (bf16[4,1,48,512]{3,2,1,0:T(8,128)(2,1)}, bf16[4,1,48,512]{3,2,1,0:T(8,128)(2,1)}, u32[]{:S(2)}, u32[]{:S(2)}) collective-permute-start(bf16[4,1,48,512]{3,2,1,0:T(8,128)(2,1)} %get-tuple-element.37), channel_id=1, source_target_pairs={{0,2},{2,4},{4,6},{6,8},{8,10},{10,12},{12,14},{1,3},{3,5},{5,7},{... | collective-permute-start | bytes 589832 | tf_op jit(solution)/shard_map/ppermute | solution.py:16
  27.6 20.5 %collective-permute-start.1 = (bf16[4,1,48,512]{3,2,1,0:T(8,128)(2,1)}, bf16[4,1,48,512]{3,2,1,0:T(8,128)(2,1)}, u32[]{:S(2)}, u32[]{:S(2)}) collective-permute-start(bf16[4,1,48,512]{3,2,1,0:T(8,128)(2,1)} %get-tuple-element.38), channel_id=1, source_target_pairs={{2,0},{4,2},{6,4},{8,6},{10,8},{12,10},{14,12},{3,1},{5,3},{7,5},{... | collective-permute-start | bytes 589832 | tf_op jit(solution)/shard_map/ppermute | solution.py:17
  30.5 4.1 %copy-start.6 = (bf16[3,3,256,256]{3,2,1,0:T(8,128)(2,1)S(1)}, bf16[3,3,256,256]{3,2,1,0:T(8,128)(2,1)}, u32[]{:S(2)}) copy-start(bf16[3,3,256,256]{3,2,1,0:T(8,128)(2,1)} %param.10) | copy-start | bytes 3538948
  36.5 15.5 %copy-start.4 = (bf16[1,4,4,48,256]{4,3,2,1,0:T(8,128)(2,1)S(1)}, bf16[1,4,4,48,256]{4,3,2,1,0:T(8,128)(2,1)}, u32[]{:S(2)}) copy-start(bf16[1,4,4,48,256]{4,3,2,1,0:T(8,128)(2,1)} %param.8) | copy-start | bytes 1179652
  37.3 6.9 %copy-start.12 = (bf16[1,1,256,256]{2,3,1,0:T(8,128)(2,1)S(1)}, bf16[1,1,256,256]{2,3,1,0:T(8,128)(2,1)}, u32[]{:S(2)}) copy-start(bf16[1,1,256,256]{2,3,1,0:T(8,128)(2,1)} %copy.30) | copy-start | bytes 393220
  38.9 9.3 %copy-start.20 = (bf16[2,4,48,256]{3,2,1,0:T(8,128)(2,1)S(1)}, bf16[2,4,48,256]{3,2,1,0:T(8,128)(2,1)}, u32[]{:S(2)}) copy-start(bf16[2,4,48,256]{3,2,1,0:T(8,128)(2,1)} %slice_bitcast_fusion) | copy-start | bytes 589828
  46.8 9.2 %collective-permute-start.7 = (bf16[2,1,48,256]{3,2,1,0:T(8,128)(2,1)}, bf16[2,1,48,256]{3,2,1,0:T(8,128)(2,1)S(1)}, u32[]{:S(2)}, u32[]{:S(2)}) collective-permute-start(bf16[2,1,48,256]{3,2,1,0:T(8,128)(2,1)} %get-tuple-element.49), channel_id=1, source_target_pairs={{18,0},{20,2},{22,4},{24,6},{26,8},{28,10},{30,12},{34,16},{36,18}... | collective-permute-start | bytes 147464 | tf_op jit(solution)/shard_map/ppermute | solution.py:36
  48.2 7.9 %collective-permute-start.6 = (bf16[2,4,48,256]{3,2,1,0:T(8,128)(2,1)S(1)}, bf16[2,4,48,256]{3,2,1,0:T(8,128)(2,1)S(1)}, u32[]{:S(2)}, u32[]{:S(2)}) collective-permute-start(bf16[2,4,48,256]{3,2,1,0:T(8,128)(2,1)S(1)} %copy-done.20), channel_id=1, source_target_pairs={{16,0},{32,16},{48,32},{64,48},{80,64},{96,80},{112,96},{128,112},... | collective-permute-start | bytes 589832 | tf_op jit(solution)/shard_map/ppermute | solution.py:25
  53.2 0.9 copy-start.19
  53.6 3.4 %copy-start.22 = (bf16[1,256,256]{1,2,0:T(8,128)(2,1)S(1)}, bf16[1,256,256]{1,2,0:T(8,128)(2,1)}, u32[]{:S(2)}) copy-start(bf16[1,256,256]{1,2,0:T(8,128)(2,1)} %copy.22) | copy-start | bytes 393220
  53.6 3.4 %copy-start.24 = (bf16[1,256,256]{1,2,0:T(8,128)(2,1)S(1)}, bf16[1,256,256]{1,2,0:T(8,128)(2,1)}, u32[]{:S(2)}) copy-start(bf16[1,256,256]{1,2,0:T(8,128)(2,1)} %copy.23) | copy-start | bytes 393220
  53.6 3.4 %copy-start.26 = (bf16[1,256,256]{1,2,0:T(8,128)(2,1)S(1)}, bf16[1,256,256]{1,2,0:T(8,128)(2,1)}, u32[]{:S(2)}) copy-start(bf16[1,256,256]{1,2,0:T(8,128)(2,1)} %copy.24) | copy-start | bytes 393220
  54.1 21.0 %collective-permute-start.3 = (bf16[2,4,48,256]{3,2,1,0:T(8,128)(2,1)S(1)}, bf16[2,4,48,256]{3,2,1,0:T(8,128)(2,1)S(1)}, u32[]{:S(2)}, u32[]{:S(2)}) collective-permute-start(bf16[2,4,48,256]{3,2,1,0:T(8,128)(2,1)S(1)} %copy-done.19), channel_id=1, source_target_pairs={{0,16},{16,32},{32,48},{48,64},{64,80},{80,96},{96,112},{112,128},... | collective-permute-start | bytes 589832 | tf_op jit(solution)/shard_map/ppermute | solution.py:25
  57.0 0.9 copy-start.18
  79.1 1.3 copy-start.10
  80.3 0.8 copy-start.14
  80.3 0.9 copy-start.16
  273.7 4.3 %copy-start.3 = (bf16[3,256,256]{2,1,0:T(8,128)(2,1)S(1)}, bf16[3,256,256]{2,1,0:T(8,128)(2,1)}, u32[]{:S(2)}) copy-start(bf16[3,256,256]{2,1,0:T(8,128)(2,1)} %param.11) | copy-start | bytes 1179652
  273.8 4.3 %copy-start.13 = (bf16[1,2,48,256]{3,2,1,0:T(8,128)(2,1)S(1)}, bf16[1,2,48,256]{3,2,1,0:T(8,128)(2,1)}, u32[]{:S(2)}) copy-start(bf16[1,2,48,256]{3,2,1,0:T(8,128)(2,1)} %get-tuple-element.53) | copy-start | bytes 147460
  273.8 4.7 %copy-start.7 = (bf16[4,2,48,256]{3,2,1,0:T(8,128)(2,1)S(1)}, bf16[4,2,48,256]{3,2,1,0:T(8,128)(2,1)}, u32[]{:S(2)}) copy-start(bf16[4,2,48,256]{3,2,1,0:T(8,128)(2,1)} %get-tuple-element.54) | copy-start | bytes 589828
  273.8 4.7 %copy-start.8 = (bf16[4,2,48,256]{3,2,1,0:T(8,128)(2,1)S(1)}, bf16[4,2,48,256]{3,2,1,0:T(8,128)(2,1)}, u32[]{:S(2)}) copy-start(bf16[4,2,48,256]{3,2,1,0:T(8,128)(2,1)} %get-tuple-element.55) | copy-start | bytes 589828
  273.8 4.7 %copy-start.9 = (bf16[4,2,48,256]{3,2,1,0:T(8,128)(2,1)S(1)}, bf16[4,2,48,256]{3,2,1,0:T(8,128)(2,1)}, u32[]{:S(2)}) copy-start(bf16[4,2,48,256]{3,2,1,0:T(8,128)(2,1)} %get-tuple-element.56) | copy-start | bytes 589828
  275.6 2.9 %copy-start.23 = (bf16[1,256,256]{1,2,0:T(8,128)(2,1)S(1)}, bf16[1,256,256]{1,2,0:T(8,128)(2,1)}, u32[]{:S(2)}) copy-start(bf16[1,256,256]{1,2,0:T(8,128)(2,1)} %copy.22) | copy-start | bytes 393220
  275.6 2.9 %copy-start.25 = (bf16[1,256,256]{1,2,0:T(8,128)(2,1)S(1)}, bf16[1,256,256]{1,2,0:T(8,128)(2,1)}, u32[]{:S(2)}) copy-start(bf16[1,256,256]{1,2,0:T(8,128)(2,1)} %copy.23) | copy-start | bytes 393220
  275.6 2.9 %copy-start.27 = (bf16[1,256,256]{1,2,0:T(8,128)(2,1)S(1)}, bf16[1,256,256]{1,2,0:T(8,128)(2,1)}, u32[]{:S(2)}) copy-start(bf16[1,256,256]{1,2,0:T(8,128)(2,1)} %copy.24) | copy-start | bytes 393220
  278.0 0.8 copy-start.21
  279.8 1.0 copy-start.5
  279.8 1.1 copy-start.11
  279.8 1.2 copy-start.15
  279.8 1.3 copy-start.17
  281.2 1.2 copy-start.1
  281.2 1.4 copy-start.28

commit v8 on v4

--- a/solution.py
+++ b/solution.py
@@ -134,10 +134,11 @@
     temporal_term = lax.dot_general(
         frame_stack, upstream.reshape(-1, channels), contract, preferred_element_type=jnp.float32
     )
-    weight_terms = jnp.concatenate([spatial_term, temporal_term], axis=0) * grad_scale
-    summed = lax.psum(weight_terms, ("tm", "height", "dp")).astype(jnp.bfloat16)
-    spatial_grad = summed[: 9 * channels].reshape(3, 3, channels, channels)
-    temporal_grad = summed[9 * channels :].reshape(3, channels, channels)
+    spatial_sum, temporal_sum = lax.psum(
+        (spatial_term * grad_scale, temporal_term * grad_scale), ("tm", "height", "dp")
+    )
+    spatial_grad = spatial_sum.astype(jnp.bfloat16).reshape(3, 3, channels, channels)
+    temporal_grad = temporal_sum.astype(jnp.bfloat16).reshape(3, channels, channels)
     return (decoded[None], input_grad[None], spatial_grad, temporal_grad)
 
 

time: 268 us -> 260 us (0.970)
  local copies, waits for them, and re-layouts: 18.7 us -> 11.3 us
  waiting for transfers between devices: 1.1 us -> 3.89 us
    slice x2 -> x0, local copies, waits for them, and re-layouts: 4.26 us -> none  [the longest x1 2.41 us: local(): spatial_grad = summed[:9 * channels].reshape(3, 3, channels, channels)]
    ppermute x2, waiting for transfers between devices: 1.09 us -> 3.88 us  [from_behind(): return lax.ppermute(block, axis, route)]
    unnamed x101 -> x71, local copies, waits for them, and re-layouts: 9.24 us -> 6.45 us
  transfers between devices with their start and end apart: 6 -> 6, of which waited for: 1 -> 1; matrix products, arithmetic and copies ran while one was open for 5% -> 4% of each run, Pallas kernels for 0% -> 0%
where the time goes in v8:
time: 260 us; the launch traced here: 259 us
  blocking collectives  205 us (79%)
  starting transfers between devices  24.2 us (9%)
  local copies, waits for them, and re-layouts  11.3 us (4%)
  matrix products  9.46 us (4%)
  other arithmetic  4.02 us (2%)
  waiting for transfers between devices  3.89 us (1%)
    psum x1, blocking collectives, local(): lax.psum((spatial_term * grad_scale, temporal_term * grad_scale), ('tm',...  205 us
    ppermute x2, starting transfers between devices, from_behind(): return lax.ppermute(block, axis, route)  15.2 us
    unnamed x71, local copies, waits for them, and re-layouts  6.45 us
    ppermute x2, starting transfers between devices, extended(): before = lax.ppermute(last, axis, up)  6.41 us
  transfers between devices with their start and end apart: 6, of which 1 were waited for; matrix products, arithmetic and copies ran while one was open for 4% of the time, Pallas kernels for 0%

profile of v8, /device:TPU:7, one launch (start us, length us, event | category | flops | bytes accessed | tf_op | source)
XLA Modules:
  0.0 259.1 jit_solution(6937136790871638325)
XLA Ops:
  0.7 1.7 slice_bitcast_fusion
  2.3 13.1 %collective-permute-start.3 = (bf16[2,4,48,256]{3,2,1,0:T(8,128)(2,1)}, bf16[2,4,48,256]{3,2,1,0:T(8,128)(2,1)S(1)}, u32[]{:S(2)}, u32[]{:S(2)}) collective-permute-start(bf16[2,4,48,256]{3,2,1,0:T(8,128)(2,1)} %slice_bitcast_fusion), channel_id=1, source_target_pairs={{16,0},{32,16},{48,32},{64,48},{80,64},{96,80},{112,96},{128,112},... | collective-permute-start | bytes 589832 | tf_op jit(solution)/shard_map/ppermute | solution.py:25
  15.5 1.6 slice_bitcast_fusion.1
  17.1 2.0 collective-permute-start.2
  19.2 1.8 pad_maximum_fusion.8
  20.9 3.2 %collective-permute-start = (bf16[4,1,48,512]{3,2,1,0:T(8,128)(2,1)}, bf16[4,1,48,512]{3,2,1,0:T(8,128)(2,1)S(1)}, u32[]{:S(2)}, u32[]{:S(2)}) collective-permute-start(bf16[4,1,48,512]{3,2,1,0:T(8,128)(2,1)} %get-tuple-element.39), channel_id=1, source_target_pairs={{0,2},{2,4},{4,6},{6,8},{8,10},{10,12},{12,14},{1,3},{3,5},{5,7},{... | collective-permute-start | bytes 589832 | tf_op jit(solution)/shard_map/ppermute | solution.py:16
  24.1 1.3 collective-permute-start.1
  25.5 0.2 fusion.75
  25.7 0.2 convolution_add_fusion.2
  25.9 0.1 fusion.92
  26.0 0.1 copy.33
  26.1 0.1 copy.32
  26.2 0.1 copy.31
  26.3 0.1 copy.30
  26.4 0.1 copy.29
  26.6 0.1 copy.28
  26.7 0.1 copy.27
  26.8 0.1 copy.26
  26.9 0.1 copy.25
  27.2 1.0 copy-done.12
  28.2 0.1 copy.22
  28.3 0.1 copy.23
  28.4 0.1 copy.24
  28.5 3.9 %collective-permute-done.2 = bf16[2,4,48,256]{3,2,1,0:T(8,128)(2,1)} collective-permute-done((bf16[2,4,48,256]{3,2,1,0:T(8,128)(2,1)}, bf16[2,4,48,256]{3,2,1,0:T(8,128)(2,1)}, u32[]{:S(2)}, u32[]{:S(2)}) %collective-permute-start.2) | collective-permute-done | bytes 196640 | tf_op jit(solution)/shard_map/ppermute | solution.py:25
  32.4 0.9 constant_dynamic-update-slice_fusion.1
  33.4 3.2 %collective-permute-start.4 = (bf16[2,1,48,512]{3,2,1,0:T(8,128)(2,1)S(1)}, bf16[2,1,48,512]{3,2,1,0:T(8,128)(2,1)S(1)}, u32[]{:S(2)}, u32[]{:S(2)}) collective-permute-start(bf16[2,1,48,512]{3,2,1,0:T(8,128)(2,1)S(1)} %get-tuple-element.50), channel_id=1, source_target_pairs={{0,2},{2,4},{4,6},{6,8},{8,10},{10,12},{12,14},{1,3},{3,5},{5,7},{... | collective-permute-start | bytes 294920 | tf_op jit(solution)/shard_map/ppermute | solution.py:16
  36.6 1.3 collective-permute-start.5
  37.9 0.1 fusion.57
  38.0 0.5 fusion.15
  38.5 0.2 fusion.71
  38.8 0.7 copy-done.3
  39.5 1.0 pad_maximum_fusion
  40.5 0.4 fusion.9
  40.9 0.1 fusion.51
  41.0 0.1 fusion.52
  41.2 0.1 fusion.53
  41.3 0.1 fusion.54
  41.4 0.1 fusion.55
  41.6 0.1 fusion.56
  41.7 1.1 convolution_multiply_fusion
  42.9 0.1 copy-done.5
  43.0 1.1 convolution_convert_fusion
  44.1 0.1 pad_maximum_fusion.1
  44.2 0.2 fusion.46
  44.4 0.4 copy-done.6
  44.8 0.5 slice-done
  45.4 0.2 fusion.78
  45.6 0.2 convolution_add_fusion.4
  45.9 0.4 copy-done.9
  46.2 0.1 copy-done.11
  46.3 0.3 fusion.64
  46.6 0.2 fusion.32
  47.3 0.6 convolution_convert_fusion.1
  47.9 0.3 fusion.42
  48.2 0.1 slice_dynamic-update-slice_fusion.5
  48.4 0.1 slice_dynamic-update-slice_fusion.3
  48.7 0.1 slice_dynamic-update-slice_fusion.1
  48.9 0.6 slice-done.1
  49.5 0.2 copy-done.7
  49.7 0.1 fusion.58
  49.7 1.2 fusion.4
  51.0 1.4 convolution_multiply_fusion.1
  52.4 1.9 fusion.5
  54.3 204.8 %all-reduce.5 = (bf16[2304,256]{1,0:T(8,128)(2,1)}, bf16[768,256]{1,0:T(8,128)(2,1)}) all-reduce(f32[2304,256]{1,0:T(8,128)S(1)} %convolution_multiply_fusion, f32[768,256]{1,0:T(8,128)} %convolution_multiply_fusion.1), channel_id=1, replica_groups=mesh['tm'=32,'height'=8,'dp'=2] {'tm','height','dp'}, use_global_device_ids=true, to_apply=%region_0.1 | all-reduce | flops 786432 | bytes 4718592 | tf_op jit(solution)/shard_map/psum | solution.py:137
  (68 shorter events, 1.1 us)
Async XLA Ops:
  0.6 24.8 %copy-start = (bf16[1,4,4,48,256]{4,3,2,1,0:T(8,128)(2,1)S(1)}, bf16[1,4,4,48,256]{4,3,2,1,0:T(8,128)(2,1)}, u32[]{:S(2)}) copy-start(bf16[1,4,4,48,256]{4,3,2,1,0:T(8,128)(2,1)} %param.9) | copy-start | bytes 1179652
  0.6 24.8 %copy-start.2 = (bf16[3,256,256]{2,1,0:T(8,128)(2,1)S(1)}, bf16[3,256,256]{2,1,0:T(8,128)(2,1)}, u32[]{:S(2)}) copy-start(bf16[3,256,256]{2,1,0:T(8,128)(2,1)} %param.11) | copy-start | bytes 1179652
  2.3 31.0 %collective-permute-start.3 = (bf16[2,4,48,256]{3,2,1,0:T(8,128)(2,1)}, bf16[2,4,48,256]{3,2,1,0:T(8,128)(2,1)S(1)}, u32[]{:S(2)}, u32[]{:S(2)}) collective-permute-start(bf16[2,4,48,256]{3,2,1,0:T(8,128)(2,1)} %slice_bitcast_fusion), channel_id=1, source_target_pairs={{16,0},{32,16},{48,32},{64,48},{80,64},{96,80},{112,96},{128,112},... | collective-permute-start | bytes 589832 | tf_op jit(solution)/shard_map/ppermute | solution.py:25
  17.1 8.8 %copy-start.4 = (bf16[3,3,256,256]{3,2,1,0:T(8,128)(2,1)S(1)}, bf16[3,3,256,256]{3,2,1,0:T(8,128)(2,1)}, u32[]{:S(2)}) copy-start(bf16[3,3,256,256]{3,2,1,0:T(8,128)(2,1)} %param.10) | copy-start | bytes 3538948
  17.1 15.3 %collective-permute-start.2 = (bf16[2,4,48,256]{3,2,1,0:T(8,128)(2,1)}, bf16[2,4,48,256]{3,2,1,0:T(8,128)(2,1)}, u32[]{:S(2)}, u32[]{:S(2)}) collective-permute-start(bf16[2,4,48,256]{3,2,1,0:T(8,128)(2,1)} %slice_bitcast_fusion.1), channel_id=1, source_target_pairs={{0,16},{16,32},{32,48},{48,64},{64,80},{80,96},{96,112},{112,128},... | collective-permute-start | bytes 589832 | tf_op jit(solution)/shard_map/ppermute | solution.py:25
  20.9 17.9 %collective-permute-start = (bf16[4,1,48,512]{3,2,1,0:T(8,128)(2,1)}, bf16[4,1,48,512]{3,2,1,0:T(8,128)(2,1)S(1)}, u32[]{:S(2)}, u32[]{:S(2)}) collective-permute-start(bf16[4,1,48,512]{3,2,1,0:T(8,128)(2,1)} %get-tuple-element.39), channel_id=1, source_target_pairs={{0,2},{2,4},{4,6},{6,8},{8,10},{10,12},{12,14},{1,3},{3,5},{5,7},{... | collective-permute-start | bytes 589832 | tf_op jit(solution)/shard_map/ppermute | solution.py:16
  24.1 14.7 %collective-permute-start.1 = (bf16[4,1,48,512]{3,2,1,0:T(8,128)(2,1)S(1)}, bf16[4,1,48,512]{3,2,1,0:T(8,128)(2,1)}, u32[]{:S(2)}, u32[]{:S(2)}) collective-permute-start(bf16[4,1,48,512]{3,2,1,0:T(8,128)(2,1)S(1)} %get-tuple-element.40), channel_id=1, source_target_pairs={{2,0},{4,2},{6,4},{8,6},{10,8},{12,10},{14,12},{3,1},{5,3},{7,5},{... | collective-permute-start | bytes 589832 | tf_op jit(solution)/shard_map/ppermute | solution.py:17
  27.1 1.0 copy-start.12
  28.4 10.1 %copy-start.8 = (bf16[1,256,256]{1,2,0:T(8,128)(2,1)}, bf16[1,256,256]{1,2,0:T(8,128)(2,1)S(1)}, u32[]{:S(2)}) copy-start(bf16[1,256,256]{1,2,0:T(8,128)(2,1)S(1)} %copy.23) | copy-start | bytes 393220
  28.5 10.0 %copy-start.10 = (bf16[1,256,256]{1,2,0:T(8,128)(2,1)}, bf16[1,256,256]{1,2,0:T(8,128)(2,1)S(1)}, u32[]{:S(2)}) copy-start(bf16[1,256,256]{1,2,0:T(8,128)(2,1)S(1)} %copy.24) | copy-start | bytes 393220
  33.4 10.7 %collective-permute-start.4 = (bf16[2,1,48,512]{3,2,1,0:T(8,128)(2,1)S(1)}, bf16[2,1,48,512]{3,2,1,0:T(8,128)(2,1)S(1)}, u32[]{:S(2)}, u32[]{:S(2)}) collective-permute-start(bf16[2,1,48,512]{3,2,1,0:T(8,128)(2,1)S(1)} %get-tuple-element.50), channel_id=1, source_target_pairs={{0,2},{2,4},{4,6},{6,8},{8,10},{10,12},{12,14},{1,3},{3,5},{5,7},{... | collective-permute-start | bytes 294920 | tf_op jit(solution)/shard_map/ppermute | solution.py:16
  36.6 7.5 %collective-permute-start.5 = (bf16[2,1,48,512]{3,2,1,0:T(8,128)(2,1)S(1)}, bf16[2,1,48,512]{3,2,1,0:T(8,128)(2,1)S(1)}, u32[]{:S(2)}, u32[]{:S(2)}) collective-permute-start(bf16[2,1,48,512]{3,2,1,0:T(8,128)(2,1)S(1)} %get-tuple-element.51), channel_id=1, source_target_pairs={{2,0},{4,2},{6,4},{8,6},{10,8},{12,10},{14,12},{3,1},{5,3},{7,5},{... | collective-permute-start | bytes 294920 | tf_op jit(solution)/shard_map/ppermute | solution.py:17
  38.5 1.0 copy-start.3
  40.5 3.6 %copy-start.1 = (bf16[4,6,48,512]{3,2,1,0:T(8,128)(2,1)}, bf16[4,6,48,512]{3,2,1,0:T(8,128)(2,1)S(1)}, u32[]{:S(2)}) copy-start(bf16[4,6,48,512]{3,2,1,0:T(8,128)(2,1)S(1)} %pad_maximum_fusion) | copy-start | bytes 3538948
  41.7 1.3 copy-start.5
  44.1 0.7 copy-start.6
  44.1 1.2 slice-start
  45.3 0.9 copy-start.9
  45.3 1.0 copy-start.11
  48.6 0.9 slice-start.1
  48.6 1.1 copy-start.7
  51.0 1.4 copy-start.13

commit v9 on v8

--- a/solution.py
+++ b/solution.py
@@ -71,8 +71,8 @@
     )
     temporal_back = jnp.concatenate([w_temporal[2].T, w_temporal[1].T, w_temporal[0].T], axis=0)
     first_shard = lax.axis_index("tm") == 0
-    inputs_prev = from_behind(inputs[frame_count - 2 :], "tm", 1)
-    upstream_next = from_behind(upstream[:2], "tm", -1)
+    inputs_prev = from_behind(inputs, "tm", 1)[frame_count - 2 :]
+    upstream_next = from_behind(upstream, "tm", -1)[:2]
     local_both = extended(jnp.concatenate([inputs, upstream], axis=-1), (("height", 1),), 1)
     rim_both = extended(
         jnp.concatenate([inputs_prev, upstream_next], axis=-1), (("height", 1),), 1

time: 260 us -> 278 us (1.069)
  local copies, waits for them, and re-layouts: 11.3 us -> 22.1 us
  blocking collectives: 205 us -> 212 us
    unnamed x71 -> x70, local copies, waits for them, and re-layouts: 6.45 us -> 16.8 us
    psum x1, blocking collectives: 205 us -> 212 us  [local(): lax.psum((spatial_term * grad_scale, temporal_term * grad_scale), ('tm',...]
    ppermute x2, waiting for transfers between devices: 3.88 us -> 0.01 us  [from_behind(): return lax.ppermute(block, axis, route)]
  transfers between devices with their start and end apart: 6 -> 6, of which waited for: 1 -> 1; matrix products, arithmetic and copies ran while one was open for 4% -> 9% of each run, Pallas kernels for 0% -> 0%
where the time goes in v9:
time: 278 us; the launch traced here: 276 us
  blocking collectives  212 us (76%)
  starting transfers between devices  25.8 us (9%)
  local copies, waits for them, and re-layouts  22.1 us (8%)
  matrix products  9.46 us (3%)
  other arithmetic  4.17 us (2%)
    psum x1, blocking collectives, local(): lax.psum((spatial_term * grad_scale, temporal_term * grad_scale), ('tm',...  212 us
    unnamed x70, local copies, waits for them, and re-layouts  16.8 us
    ppermute x2, starting transfers between devices, from_behind(): return lax.ppermute(block, axis, route)  15.2 us
    ppermute x2, starting transfers between devices, extended(): before = lax.ppermute(last, axis, up)  8.01 us
  transfers between devices with their start and end apart: 6, of which 1 were waited for; matrix products, arithmetic and copies ran while one was open for 9% of the time, Pallas kernels for 0%

profile of v9, /device:TPU:7, one launch (start us, length us, event | category | flops | bytes accessed | tf_op | source)
XLA Modules:
  0.0 276.1 jit_solution(7806548196787086305)
XLA Ops:
  0.6 3.7 %collective-permute-start.2 = (bf16[4,4,48,256]{3,2,1,0:T(8,128)(2,1)}, bf16[4,4,48,256]{3,2,1,0:T(8,128)(2,1)}, u32[]{:S(2)}, u32[]{:S(2)}) collective-permute-start(bf16[4,4,48,256]{3,2,1,0:T(8,128)(2,1)} %bitcast.148), channel_id=1, source_target_pairs={{0,16},{16,32},{32,48},{48,64},{64,80},{80,96},{96,112},{112,128},... | collective-permute-start | bytes 1179656 | tf_op jit(solution)/shard_map/ppermute | solution.py:25
  4.3 11.5 %collective-permute-start.3 = (bf16[4,4,48,256]{3,2,1,0:T(8,128)(2,1)}, bf16[4,4,48,256]{3,2,1,0:T(8,128)(2,1)}, u32[]{:S(2)}, u32[]{:S(2)}) collective-permute-start(bf16[4,4,48,256]{3,2,1,0:T(8,128)(2,1)} %bitcast.141), channel_id=1, source_target_pairs={{16,0},{32,16},{48,32},{64,48},{80,64},{96,80},{112,96},{128,112},... | collective-permute-start | bytes 1179656 | tf_op jit(solution)/shard_map/ppermute | solution.py:25
  15.9 1.8 pad_maximum_fusion.8
  17.7 4.0 %collective-permute-start = (bf16[4,1,48,512]{3,2,1,0:T(8,128)(2,1)}, bf16[4,1,48,512]{3,2,1,0:T(8,128)(2,1)}, u32[]{:S(2)}, u32[]{:S(2)}) collective-permute-start(bf16[4,1,48,512]{3,2,1,0:T(8,128)(2,1)} %get-tuple-element.39), channel_id=1, source_target_pairs={{0,2},{2,4},{4,6},{6,8},{8,10},{10,12},{12,14},{1,3},{3,5},{5,7},{... | collective-permute-start | bytes 589832 | tf_op jit(solution)/shard_map/ppermute | solution.py:16
  21.7 1.3 collective-permute-start.1
  23.0 1.6 fusion.92
  24.6 0.2 fusion.76
  24.8 0.2 convolution_add_fusion.2
  25.1 0.8 copy.22
  25.8 0.7 copy.23
  26.6 0.8 copy.24
  27.4 0.1 copy.33
  27.5 0.1 copy.32
  27.6 0.1 copy.31
  27.7 0.8 copy.30
  28.5 0.8 copy.29
  29.3 0.8 copy.28
  30.0 0.8 copy.27
  30.8 0.1 copy.26
  30.9 0.1 copy.25
  31.0 0.7 bitcast_dynamic-update-slice_fusion.8
  31.7 0.7 bitcast_dynamic-update-slice_fusion.7
  32.3 1.6 bitcast_dynamic-update-slice_fusion.6
  33.9 1.6 bitcast_dynamic-update-slice_fusion.5
  35.5 1.6 bitcast_dynamic-update-slice_fusion.4
  37.0 0.7 bitcast_dynamic-update-slice_fusion.3
  37.7 0.7 bitcast_dynamic-update-slice_fusion.2
  38.4 0.7 bitcast_dynamic-update-slice_fusion.1
  39.0 0.7 bitcast_dynamic-update-slice_fusion
  39.7 1.1 pad_maximum_fusion
  40.9 0.4 fusion.9
  41.3 0.1 fusion.53
  41.4 0.1 fusion.54
  41.5 0.1 fusion.55
  41.7 0.1 fusion.56
  41.8 0.1 fusion.57
  42.0 0.1 fusion.58
  42.1 1.1 convolution_convert_fusion
  43.2 1.1 slice.329
  44.5 0.9 slice.328
  45.4 4.0 %collective-permute-start.4 = (bf16[2,1,48,512]{3,2,1,0:T(8,128)(2,1)S(1)}, bf16[2,1,48,512]{3,2,1,0:T(8,128)(2,1)S(1)}, u32[]{:S(2)}, u32[]{:S(2)}) collective-permute-start(bf16[2,1,48,512]{3,2,1,0:T(8,128)(2,1)S(1)} %get-tuple-element.50), channel_id=1, source_target_pairs={{0,2},{2,4},{4,6},{6,8},{8,10},{10,12},{12,14},{1,3},{3,5},{5,7},{... | collective-permute-start | bytes 294920 | tf_op jit(solution)/shard_map/ppermute | solution.py:16
  49.4 1.3 collective-permute-start.5
  50.8 0.5 fusion.15
  51.2 0.4 copy-done.9
  51.6 0.2 fusion.30
  51.9 1.1 convolution_multiply_fusion
  53.1 1.7 collective-permute-done.5
  54.8 0.2 fusion.48
  55.2 0.2 fusion.79
  55.3 0.2 convolution_add_fusion.4
  55.6 0.3 fusion.66
  55.9 0.2 fusion.34
  56.6 0.9 copy-done.5
  57.5 0.6 convolution_convert_fusion.1
  58.2 0.3 fusion.44
  58.5 0.1 slice_dynamic-update-slice_fusion.5
  58.7 0.1 slice_dynamic-update-slice_fusion.3
  58.9 0.1 slice_dynamic-update-slice_fusion.1
  59.1 0.6 slice-done.1
  59.7 0.2 copy-done.7
  60.0 1.2 fusion.4
  61.2 1.4 convolution_multiply_fusion.1
  62.6 1.9 fusion.5
  64.5 211.5 %all-reduce.5 = (bf16[2304,256]{1,0:T(8,128)(2,1)}, bf16[768,256]{1,0:T(8,128)(2,1)}) all-reduce(f32[2304,256]{1,0:T(8,128)S(1)} %convolution_multiply_fusion, f32[768,256]{1,0:T(8,128)} %convolution_multiply_fusion.1), channel_id=1, replica_groups=mesh['tm'=32,'height'=8,'dp'=2] {'tm','height','dp'}, use_global_device_ids=true, to_apply=%region_0.1 | all-reduce | flops 786432 | bytes 4718592 | tf_op jit(solution)/shard_map/psum | solution.py:137
  (66 shorter events, 1.2 us)
Async XLA Ops:
  0.6 24.0 %copy-start.2 = (bf16[3,256,256]{2,1,0:T(8,128)(2,1)S(1)}, bf16[3,256,256]{2,1,0:T(8,128)(2,1)}, u32[]{:S(2)}) copy-start(bf16[3,256,256]{2,1,0:T(8,128)(2,1)} %param.11) | copy-start | bytes 1179652
  0.6 43.8 %collective-permute-start.2 = (bf16[4,4,48,256]{3,2,1,0:T(8,128)(2,1)}, bf16[4,4,48,256]{3,2,1,0:T(8,128)(2,1)}, u32[]{:S(2)}, u32[]{:S(2)}) collective-permute-start(bf16[4,4,48,256]{3,2,1,0:T(8,128)(2,1)} %bitcast.148), channel_id=1, source_target_pairs={{0,16},{16,32},{32,48},{48,64},{64,80},{80,96},{96,112},{112,128},... | collective-permute-start | bytes 1179656 | tf_op jit(solution)/shard_map/ppermute | solution.py:25
  4.3 38.9 %collective-permute-start.3 = (bf16[4,4,48,256]{3,2,1,0:T(8,128)(2,1)}, bf16[4,4,48,256]{3,2,1,0:T(8,128)(2,1)}, u32[]{:S(2)}, u32[]{:S(2)}) collective-permute-start(bf16[4,4,48,256]{3,2,1,0:T(8,128)(2,1)} %bitcast.141), channel_id=1, source_target_pairs={{16,0},{32,16},{48,32},{64,48},{80,64},{96,80},{112,96},{128,112},... | collective-permute-start | bytes 1179656 | tf_op jit(solution)/shard_map/ppermute | solution.py:25
  17.7 9.7 %copy-start.4 = (bf16[3,3,256,256]{3,2,1,0:T(8,128)(2,1)S(1)}, bf16[3,3,256,256]{3,2,1,0:T(8,128)(2,1)}, u32[]{:S(2)}) copy-start(bf16[3,3,256,256]{3,2,1,0:T(8,128)(2,1)} %param.10) | copy-start | bytes 3538948
  17.7 22.0 %collective-permute-start = (bf16[4,1,48,512]{3,2,1,0:T(8,128)(2,1)}, bf16[4,1,48,512]{3,2,1,0:T(8,128)(2,1)}, u32[]{:S(2)}, u32[]{:S(2)}) collective-permute-start(bf16[4,1,48,512]{3,2,1,0:T(8,128)(2,1)} %get-tuple-element.39), channel_id=1, source_target_pairs={{0,2},{2,4},{4,6},{6,8},{8,10},{10,12},{12,14},{1,3},{3,5},{5,7},{... | collective-permute-start | bytes 589832 | tf_op jit(solution)/shard_map/ppermute | solution.py:16
  21.7 18.0 %collective-permute-start.1 = (bf16[4,1,48,512]{3,2,1,0:T(8,128)(2,1)}, bf16[4,1,48,512]{3,2,1,0:T(8,128)(2,1)}, u32[]{:S(2)}, u32[]{:S(2)}) collective-permute-start(bf16[4,1,48,512]{3,2,1,0:T(8,128)(2,1)} %get-tuple-element.40), channel_id=1, source_target_pairs={{2,0},{4,2},{6,4},{8,6},{10,8},{12,10},{14,12},{3,1},{5,3},{7,5},{... | collective-permute-start | bytes 589832 | tf_op jit(solution)/shard_map/ppermute | solution.py:17
  29.2 10.5 %copy-start = (bf16[1,4,4,48,256]{4,3,2,1,0:T(8,128)(2,1)S(1)}, bf16[1,4,4,48,256]{4,3,2,1,0:T(8,128)(2,1)}, u32[]{:S(2)}) copy-start(bf16[1,4,4,48,256]{4,3,2,1,0:T(8,128)(2,1)} %param.9) | copy-start | bytes 1179652
  29.3 10.5 %copy-start.3 = (bf16[1,4,4,48,256]{4,3,2,1,0:T(8,128)(2,1)S(1)}, bf16[1,4,4,48,256]{4,3,2,1,0:T(8,128)(2,1)}, u32[]{:S(2)}) copy-start(bf16[1,4,4,48,256]{4,3,2,1,0:T(8,128)(2,1)} %param.8) | copy-start | bytes 1179652
  30.0 7.0 %copy-start.8 = (bf16[1,1,256,256]{2,3,1,0:T(8,128)(2,1)S(1)}, bf16[1,1,256,256]{2,3,1,0:T(8,128)(2,1)}, u32[]{:S(2)}) copy-start(bf16[1,1,256,256]{2,3,1,0:T(8,128)(2,1)} %copy.30) | copy-start | bytes 393220
  40.9 1.2 copy-start.1
  43.2 8.1 %copy-start.6 = (bf16[768,256]{1,0:T(8,128)(2,1)}, bf16[768,256]{1,0:T(8,128)(2,1)S(1)}, u32[]{:S(2)}) copy-start(bf16[768,256]{1,0:T(8,128)(2,1)S(1)} %convolution_convert_fusion) | copy-start | bytes 1179652
  43.2 7.5 %copy-start.10 = (bf16[1,256,256]{1,2,0:T(8,128)(2,1)S(1)}, bf16[1,256,256]{1,2,0:T(8,128)(2,1)}, u32[]{:S(2)}) copy-start(bf16[1,256,256]{1,2,0:T(8,128)(2,1)} %copy.22) | copy-start | bytes 393220
  43.2 7.5 %copy-start.11 = (bf16[1,256,256]{1,2,0:T(8,128)(2,1)S(1)}, bf16[1,256,256]{1,2,0:T(8,128)(2,1)}, u32[]{:S(2)}) copy-start(bf16[1,256,256]{1,2,0:T(8,128)(2,1)} %copy.23) | copy-start | bytes 393220
  43.2 7.5 %copy-start.12 = (bf16[1,256,256]{1,2,0:T(8,128)(2,1)S(1)}, bf16[1,256,256]{1,2,0:T(8,128)(2,1)}, u32[]{:S(2)}) copy-start(bf16[1,256,256]{1,2,0:T(8,128)(2,1)} %copy.24) | copy-start | bytes 393220
  45.4 7.7 %collective-permute-start.4 = (bf16[2,1,48,512]{3,2,1,0:T(8,128)(2,1)S(1)}, bf16[2,1,48,512]{3,2,1,0:T(8,128)(2,1)S(1)}, u32[]{:S(2)}, u32[]{:S(2)}) collective-permute-start(bf16[2,1,48,512]{3,2,1,0:T(8,128)(2,1)S(1)} %get-tuple-element.50), channel_id=1, source_target_pairs={{0,2},{2,4},{4,6},{6,8},{8,10},{10,12},{12,14},{1,3},{3,5},{5,7},{... | collective-permute-start | bytes 294920 | tf_op jit(solution)/shard_map/ppermute | solution.py:16
  49.4 5.4 %collective-permute-start.5 = (bf16[2,1,48,512]{3,2,1,0:T(8,128)(2,1)S(1)}, bf16[2,1,48,512]{3,2,1,0:T(8,128)(2,1)S(1)}, u32[]{:S(2)}, u32[]{:S(2)}) collective-permute-start(bf16[2,1,48,512]{3,2,1,0:T(8,128)(2,1)S(1)} %get-tuple-element.51), channel_id=1, source_target_pairs={{2,0},{4,2},{6,4},{8,6},{10,8},{12,10},{14,12},{3,1},{5,3},{7,5},{... | collective-permute-start | bytes 294920 | tf_op jit(solution)/shard_map/ppermute | solution.py:17
  50.7 0.9 copy-start.9
  53.1 2.0 slice-start
  56.2 1.3 copy-start.5
  58.8 0.9 slice-start.1
  58.8 1.1 copy-start.7
  61.2 1.4 copy-start.13
